TPU v7x, 256 devices: a whole 4x4x8 slice. The times are simulated.
256 devices in a mesh: win: 8 (over x_hi, y), tx: 8 (over z), ty: 4 (over x_lo, core).
Axes of the slice: x: 4 (x_hi: 2, x_lo: 2; x = x_hi * 2 + x_lo), y: 4, z: 8, core: 2. Of those that a mesh axis runs over, the one named last changes fastest.
Arguments:
- dual: float32 [8, 4, 4, 256, 1024], P('win', None, None, 'ty', 'tx'), may hold values from -6 to 6
- obs_dual: float32 [8, 2, 256, 1024], P('win', None, 'ty', 'tx'), may hold values from -6 to 6
- increment: float32 [8, 4, 4, 256, 1024], P('win', None, None, 'ty', 'tx'), may hold values from -6 to 6
- trajectory: float32 [8, 3, 2, 4, 256, 1024], P('win', None, None, None, 'ty', 'tx'), may hold values from -0.3 to 0.3
- diffusion: float32 [4, 4], replicated, may hold values from 0.01 to 0.045
- obs_weight: float32 [2, 4, 4], replicated, may hold values from -1.5 to 1.5
- model_var: float32 [8, 4, 4, 256, 1024], P('win', None, None, 'ty', 'tx'), may hold values from 0.3 to 3
- obs_var: float32 [8, 2, 256, 1024], P('win', None, 'ty', 'tx'), may hold values from 0.5 to 2
Outputs:
- next_dual: float32 [8, 4, 4, 256, 1024], P('win', None, None, 'ty', 'tx')
- next_obs: float32 [8, 2, 256, 1024], P('win', None, 'ty', 'tx')
- next_increment: float32 [8, 4, 4, 256, 1024], P('win', None, None, 'ty', 'tx')
- coeffs: float32 [2], replicated
All inputs are finite; a program needn't handle non-finite values.
Results may differ from a plain program's by a relative error of at most 0.00016.
Values sent between devices are 32-bit elements; how exact they have to be, the bound alone decides.
No kernel may reach another device: no remote copies, remote signals or barrier semaphores. Data moves between devices by JAX's collectives and lax.ppermute only.
A program may use at most 128 MiB of HBM per device.

v0:
```python
import jax
import jax.numpy as jnp
from jax import lax
from jax.sharding import PartitionSpec as P


def padded_2(value, sides, width):
    for axis, dim in sides:
        size, length = (lax.axis_size(axis), value.shape[dim])
        up = [(i, (i + 1) % size) for i in range(size)]
        down = [(j, i) for i, j in up]
        last = lax.slice_in_dim(value, length - width, length, axis=dim)
        leading = lax.slice_in_dim(value, 0, width, axis=dim)
        before = lax.ppermute(last, axis, up)
        after = lax.ppermute(leading, axis, down)
        value = jnp.concatenate([before, value, after], axis=dim)
    return value


def from_behind(block, axis, distance):
    devices = range(lax.axis_size(axis))
    route = [(i - distance, i) for i in devices if i - distance in devices]
    return lax.ppermute(block, axis, route)


def prefix(value, axis, combine, identity, reverse):
    size, position = (lax.axis_size(axis), lax.axis_index(axis))
    everything = lax.all_gather(value, axis)
    start = jnp.broadcast_to(jnp.asarray(identity, value.dtype), value.shape)

    def lap(k, before):
        at = size - 1 - k if reverse else k
        reached = at > position if reverse else at < position
        new = combine(before, everything[at])
        return jnp.where(reached, new, before)

    return lax.fori_loop(0, size, lap, start)


def trimmed(padded):
    row_index = lax.axis_index("ty")
    last_row = lax.axis_size("ty") - 1
    rows = padded.shape[-2] - 2
    places = jnp.arange(rows)
    keep_north = jnp.where((places == rows - 1) & (row_index == last_row), 0.0, 1.0).astype(
        padded.dtype
    )[:, None]
    keep_south = jnp.where((places == 0) & (row_index == 0), 0.0, 1.0).astype(padded.dtype)[:, None]
    east = padded[..., 1:-1, 2:]
    west = padded[..., 1:-1, :-2]
    north = padded[..., 2:, 1:-1] * keep_north
    south = padded[..., :-2, 1:-1] * keep_south
    return (east, west, north, south)


def forward_step(field, wind_lon, wind_lat, diffuse):
    pos_lon = jnp.maximum(wind_lon, 0.0)[None]
    neg_lon = jnp.minimum(wind_lon, 0.0)[None]
    pos_lat = jnp.maximum(wind_lat, 0.0)[None]
    neg_lat = jnp.minimum(wind_lat, 0.0)[None]
    padded = padded_2(field, (("tx", 3), ("ty", 2)), 1)
    east, west, north, south = trimmed(padded)
    return (
        field
        - pos_lon * (field - west)
        - neg_lon * (east - field)
        - pos_lat * (field - south)
        - neg_lat * (north - field)
        + diffuse * (east + west + north + south - 4.0 * field)
    )


def back_from_terms(field, wind_lon, wind_lat, diffuse):
    pos_lon = jnp.maximum(wind_lon, 0.0)[None]
    neg_lon = jnp.minimum(wind_lon, 0.0)[None]
    pos_lat = jnp.maximum(wind_lat, 0.0)[None]
    neg_lat = jnp.minimum(wind_lat, 0.0)[None]
    stacked = jnp.stack([field, pos_lon * field, neg_lon * field, pos_lat * field, neg_lat * field])
    padded = padded_2(stacked, (("tx", 4), ("ty", 3)), 1)
    east, west, north, south = trimmed(padded)
    diagonal = 1.0 - pos_lon + neg_lon - pos_lat + neg_lat - 4.0 * diffuse
    return (
        diagonal * field
        + east[1]
        - west[2]
        + north[3]
        - south[4]
        + diffuse * (east[0] + west[0] + north[0] + south[0])
    )


def add_terms(earlier, later):
    return earlier + later


def per_device(dual, obs_dual, increment, trajectory, diffusion, obs_weight, model_var, obs_var):
    multipliers = dual[0]
    observed = obs_dual[0]
    state = increment[0]
    winds = trajectory[0]
    variance = model_var[0]
    obs_variance = obs_var[0]
    diffuse = diffusion[:, :, None, None]
    steps = winds.shape[0]
    following = from_behind(multipliers, "win", -1)
    adjoint_start = (
        jnp.einsum("ofl,oab->flab", obs_weight, observed, precision=lax.Precision.HIGHEST)
        - following
    )
    moved = state
    for index in range(steps):
        moved = forward_step(moved, winds[index, 0], winds[index, 1], diffuse)
    adjoint_field = adjoint_start
    for index in reversed(range(steps)):
        adjoint_field = back_from_terms(adjoint_field, winds[index, 0], winds[index, 1], diffuse)
    carried = from_behind(moved, "win", 1)
    obs_end = jnp.einsum("ofl,flab->oab", obs_weight, moved, precision=lax.Precision.HIGHEST)
    zl = variance * multipliers + state - carried
    zm = obs_variance * observed + obs_end
    zd = multipliers + adjoint_field
    zeros = jnp.zeros_like(zd)
    later_sum = prefix(zd, "win", add_terms, zeros, True)
    new_lam = later_sum + zd
    source = zl - variance * new_lam
    new_state = prefix(source, "win", add_terms, zeros, False) + source
    new_obs = zm / obs_variance
    local_inner = (
        jnp.sum(new_lam * multipliers) + jnp.sum(new_obs * observed) + jnp.sum(new_state * state)
    )
    local_square = (
        jnp.sum(multipliers * multipliers) + jnp.sum(observed * observed) + jnp.sum(state * state)
    )
    inner, square = lax.psum((local_inner, local_square), ("win", "tx", "ty"))
    coeff = inner / square
    rest_lam = new_lam - coeff * multipliers
    rest_obs = new_obs - coeff * observed
    rest_state = new_state - coeff * state
    local_rest = (
        jnp.sum(rest_lam * rest_lam)
        + jnp.sum(rest_obs * rest_obs)
        + jnp.sum(rest_state * rest_state)
    )
    rest_sq = lax.psum(local_rest, ("win", "tx", "ty"))
    count = (
        (multipliers.size * 2 + observed.size)
        * lax.axis_size("win")
        * lax.axis_size("tx")
        * lax.axis_size("ty")
    )
    scale = jnp.sqrt(rest_sq / count + 1e-06)
    return (
        (rest_lam / scale)[None],
        (rest_obs / scale)[None],
        (rest_state / scale)[None],
        jnp.stack([coeff, scale]),
    )


def solution(mesh):
    in_specs = (
        P("win", None, None, "ty", "tx"),
        P("win", None, "ty", "tx"),
        P("win", None, None, "ty", "tx"),
        P("win", None, None, None, "ty", "tx"),
        P(),
        P(),
        P("win", None, None, "ty", "tx"),
        P("win", None, "ty", "tx"),
    )
    out_specs = (
        P("win", None, None, "ty", "tx"),
        P("win", None, "ty", "tx"),
        P("win", None, None, "ty", "tx"),
        P(),
    )
    return jax.shard_map(
        per_device, mesh=mesh, in_specs=in_specs, out_specs=out_specs, check_vma=False
    )
```

profile of v0, /device:TPU:1, one launch (start us, length us, event | category | flops | bytes accessed | tf_op | source)
XLA Modules:
  0.0 468.2 jit_solution(4594419644307913672)
XLA Ops:
  13.4 8.8 %collective-permute-done = f32[4,4,64,128]{3,1,2,0:T(4,128)S(1)} collective-permute-done((f32[4,4,64,128]{3,1,2,0:T(4,128)S(1)}, f32[4,4,64,128]{3,1,2,0:T(4,128)S(1)}, u32[]{:S(2)}, u32[]{:S(2)}) %collective-permute-start) | collective-permute-done | bytes 524320 | tf_op jit(solution)/shard_map/ppermute | solution.py:23
  23.9 3.9 fusion.53
  30.6 7.6 %collective-permute-start.1 = (f32[5,4,4,64,1]{3,2,4,1,0:T(4,128)}, f32[5,4,4,64,1]{3,2,4,1,0:T(4,128)}, u32[]{:S(2)}, u32[]{:S(2)}) collective-permute-start(f32[5,4,4,64,1]{3,2,4,1,0:T(4,128)} %copy.52), channel_id=1, source_target_pairs={{4,0},{8,4},{12,8},{16,12},{20,16},{24,20},{28,24},{0,28},{5,1},{9... | collective-permute-start | bytes 61448 | tf_op jit(solution)/shard_map/ppermute | solution.py:15
  45.4 2.8 copy.55
  49.5 3.0 collective-permute-start.3
  56.5 4.7 %fusion.5 = (f32[5,4,4,64,128]{4,2,3,1,0:T(4,128)S(1)}, f32[5,4,4,64,128]{4,2,3,1,0:T(4,128)S(1)}) fusion(f32[5,4,4,1,130]{4,2,3,1,0:T(4,128)S(1)} %collective-permute-done.3, f32[5,4,4,64,1]{4,2,3,1,0:T(4,128)S(1)} %copy-done.3, f32[5,4,4,64,128]{4,2,3,1,0:T(4,128)S(1)} %bitcast_dynamic-update-slice_fusion.10, f32[5,4,4,64,1]{4,2,3,1,0:T(4,128)S(1)} %copy-done.4, ...), kind=kLoop, calls=%fused_computation.23 | loop fusion | flops 5242880 | bytes 7988992 | tf_op jit(solution)/shard_map/mul | solution.py:51
  61.2 3.2 bitcast_dynamic-update-slice_fusion.9
  65.4 3.9 fusion.52
  87.3 4.7 %fusion.3 = (f32[5,4,4,64,128]{4,2,3,1,0:T(4,128)S(1)}, f32[5,4,4,64,128]{4,2,3,1,0:T(4,128)S(1)}) fusion(f32[5,4,4,1,130]{4,2,3,1,0:T(4,128)S(1)} %collective-permute-done.7, f32[5,4,4,64,1]{4,2,3,1,0:T(4,128)S(1)} %copy-done.5, f32[5,4,4,64,128]{4,2,3,1,0:T(4,128)S(1)} %bitcast_dynamic-update-slice_fusion.5, f32[5,4,4,64,1]{4,2,3,1,0:T(4,128)S(1)} %copy-done.6, ...), kind=kLoop, calls=%fused_computation.15 | loop fusion | flops 5242880 | bytes 7988992 | tf_op jit(solution)/shard_map/mul | solution.py:51
  94.7 3.1 fusion.51
  113.9 4.7 %fusion.1 = (f32[5,4,4,64,128]{4,2,3,1,0:T(4,128)S(1)}, f32[5,4,4,64,128]{4,2,3,1,0:T(4,128)S(1)}) fusion(f32[5,4,4,1,130]{4,2,3,1,0:T(4,128)S(1)} %collective-permute-done.11, f32[5,4,4,64,1]{4,2,3,1,0:T(4,128)S(1)} %copy-done.7, f32[5,4,4,64,128]{4,2,3,1,0:T(4,128)S(1)} %copy-done.1, f32[5,4,4,64,1]{4,2,3,1,0:T(4,128)S(1)} %copy-done.8, ...), kind=kLoop, calls=%fused_computation.7 | loop fusion | flops 5242880 | bytes 7988992 | tf_op jit(solution)/shard_map/mul | solution.py:51
  126.8 10.8 %collective-permute-done.13 = f32[4,4,64,1]{3,1,2,0:T(4,128)S(1)} collective-permute-done((f32[4,4,64,1]{3,1,2,0:T(4,128)S(1)}, f32[4,4,64,1]{3,1,2,0:T(4,128)S(1)}, u32[]{:S(2)}, u32[]{:S(2)}) %collective-permute-start.13) | collective-permute-done | bytes 4128 | tf_op jit(solution)/shard_map/ppermute | solution.py:14
  137.7 3.1 collective-permute-start.15
  149.7 11.4 %collective-permute-done.17 = f32[4,4,64,1]{3,1,2,0:T(4,128)S(1)} collective-permute-done((f32[4,4,64,1]{3,1,2,0:T(4,128)S(1)}, f32[4,4,64,1]{3,1,2,0:T(4,128)S(1)}, u32[]{:S(2)}, u32[]{:S(2)}) %collective-permute-start.17) | collective-permute-done | bytes 4128 | tf_op jit(solution)/shard_map/ppermute | solution.py:14
  163.4 3.3 collective-permute-done.20
  169.2 3.3 collective-permute-start.22
  172.4 10.7 %collective-permute-done.21 = f32[4,4,64,1]{3,1,2,0:T(4,128)S(1)} collective-permute-done((f32[4,4,64,1]{3,1,2,0:T(4,128)S(1)}, f32[4,4,64,1]{3,1,2,0:T(4,128)S(1)}, u32[]{:S(2)}, u32[]{:S(2)}) %collective-permute-start.21) | collective-permute-done | bytes 4128 | tf_op jit(solution)/shard_map/ppermute | solution.py:14
  188.3 3.5 multiply_add_fusion
  191.9 3.3 collective-permute-start.25
  197.5 10.1 %while.30 = (s32[]{:T(128)}, f32[4,4,64,128]{3,2,1,0:T(8,128)S(1)}, s32[]{:T(128)}, f32[8,4,4,64,128]{4,3,2,1,0:T(8,128)}, s32[]{:T(128)}, /*index=5*/s32[]{:T(128)}, s32[]{:T(128)}, s32[]{:T(128)}) while((s32[]{:T(128)}, f32[4,4,64,128]{3,2,1,0:T(8,128)S(1)}, s32[]{:T(128)}, f32[8,4,4,64,128]{4,3,2,1,0:T(8,128)}, s32[]{:T(128)}, ...), condition=%wide.region_1.2_spmd.clone, body=%wide.region_0.1_spmd.clone.sunk | while | flops 393224 | bytes 1573019 | solution.py:37
  218.3 70.6 %all-gather.7.cloned.1.call-done = f32[32,4,64,128]{3,2,1,0:T(8,128)} async-done(((f32[4,4,64,128]{3,2,1,0:T(8,128)}), f32[32,4,64,128]{3,2,1,0:T(8,128)}) %all-gather.7.cloned.1.call-update) | async-done | bytes 4194320 | tf_op jit(solution)/shard_map/all_gather | solution.py:28
  288.9 10.0 %while.31 = (s32[]{:T(128)}, f32[4,4,64,128]{3,2,1,0:T(8,128)S(1)}, s32[]{:T(128)}, f32[8,4,4,64,128]{4,3,2,1,0:T(8,128)}, s32[]{:T(128)}, /*index=5*/s32[]{:T(128)}) while((s32[]{:T(128)}, f32[4,4,64,128]{3,2,1,0:T(8,128)S(1)}, s32[]{:T(128)}, f32[8,4,4,64,128]{4,3,2,1,0:T(8,128)}, s32[]{:T(128)}, /*index=5*/s32[]{:T(128)}) %tuple.124), condition=%wide.region_5.6_spmd.clone, body=%wide.region_4.5_spmd.clone.sunk | while | flops 393220 | bytes 1572957 | solution.py:37
  301.6 74.7 %all-reduce = (f32[]{:T(128)}, f32[]{:T(128)}) all-reduce(f32[]{:T(128)S(6)} %add.308, f32[]{:T(128)S(6)} %add.310), channel_id=1, replica_groups=mesh['win'=8,'tx'=8,'ty'=4] {'win','tx','ty'}, use_global_device_ids=true, to_apply=%region_7.8 | all-reduce | flops 2 | bytes 16 | tf_op jit(solution)/shard_map/psum | solution.py:133
  382.5 74.1 %psum.23 = f32[]{:T(128)} all-reduce(f32[]{:T(128)S(6)} %add.312), channel_id=1, replica_groups=mesh['win'=8,'tx'=8,'ty'=4] {'win','tx','ty'}, use_global_device_ids=true, to_apply=%region_15.16 | all-reduce | flops 1 | bytes 8 | tf_op jit(solution)/shard_map/psum | solution.py:143
  (245 shorter events, 124.9 us)
Async XLA Ops:
  7.2 190.3 %all-gather.5.cloned.1.call-start = ((), (), s32[]{:S(2)}) async-start(), calls=%async_computation | async-start | bytes 4718592 | tf_op jit(solution)/shard_map/all_gather | solution.py:28
  8.7 13.5 %collective-permute-start = (f32[4,4,64,128]{3,1,2,0:T(4,128)S(1)}, f32[4,4,64,128]{3,1,2,0:T(4,128)S(1)}, u32[]{:S(2)}, u32[]{:S(2)}) collective-permute-start(f32[4,4,64,128]{3,1,2,0:T(4,128)S(1)} %bitcast.280), channel_id=1, source_target_pairs={{32,0},{64,32},{96,64},{128,96},{160,128},{192,160},{224,192},{33,... | collective-permute-start | bytes 1572872 | tf_op jit(solution)/shard_map/ppermute | solution.py:23
  30.6 10.4 %collective-permute-start.1 = (f32[5,4,4,64,1]{3,2,4,1,0:T(4,128)}, f32[5,4,4,64,1]{3,2,4,1,0:T(4,128)}, u32[]{:S(2)}, u32[]{:S(2)}) collective-permute-start(f32[5,4,4,64,1]{3,2,4,1,0:T(4,128)} %copy.52), channel_id=1, source_target_pairs={{4,0},{8,4},{12,8},{16,12},{20,16},{24,20},{28,24},{0,28},{5,1},{9... | collective-permute-start | bytes 61448 | tf_op jit(solution)/shard_map/ppermute | solution.py:15
  41.1 4.4 collective-permute-start.2
  49.5 6.9 %collective-permute-start.3 = (f32[5,4,4,1,130]{4,2,3,1,0:T(4,128)S(1)}, f32[5,4,4,1,130]{4,2,3,1,0:T(4,128)S(1)}, u32[]{:S(2)}, u32[]{:S(2)}) collective-permute-start(f32[5,4,4,1,130]{4,2,3,1,0:T(4,128)S(1)} %get-tuple-element.283), channel_id=1, source_target_pairs={{1,0},{2,1},{3,2},{0,3},{5,4},{6,5},{7,6},{4,7},{9,8},{10,9},{11,1... | collective-permute-start | bytes 124808 | tf_op jit(solution)/shard_map/ppermute | solution.py:15
  52.6 3.9 collective-permute-start.4
  71.5 3.8 collective-permute-start.5
  74.1 4.1 collective-permute-start.6
  81.5 5.8 %collective-permute-start.7 = (f32[5,4,4,1,130]{4,2,3,1,0:T(4,128)S(1)}, f32[5,4,4,1,130]{4,2,3,1,0:T(4,128)S(1)}, u32[]{:S(2)}, u32[]{:S(2)}) collective-permute-start(f32[5,4,4,1,130]{4,2,3,1,0:T(4,128)S(1)} %get-tuple-element.279), channel_id=1, source_target_pairs={{1,0},{2,1},{3,2},{0,3},{5,4},{6,5},{7,6},{4,7},{9,8},{10,9},{11,1... | collective-permute-start | bytes 124808 | tf_op jit(solution)/shard_map/ppermute | solution.py:15
  83.9 3.4 collective-permute-start.8
  101.2 4.1 collective-permute-start.10
  108.7 5.2 %collective-permute-start.11 = (f32[5,4,4,1,130]{4,2,3,1,0:T(4,128)S(1)}, f32[5,4,4,1,130]{4,2,3,1,0:T(4,128)S(1)}, u32[]{:S(2)}, u32[]{:S(2)}) collective-permute-start(f32[5,4,4,1,130]{4,2,3,1,0:T(4,128)S(1)} %get-tuple-element.275), channel_id=1, source_target_pairs={{1,0},{2,1},{3,2},{0,3},{5,4},{6,5},{7,6},{4,7},{9,8},{10,9},{11,1... | collective-permute-start | bytes 124808 | tf_op jit(solution)/shard_map/ppermute | solution.py:15
  122.2 166.7 %all-gather.7.cloned.1.call-start = ((), (), s32[]{:S(2)}) async-start(), calls=%async_computation.1 | async-start | bytes 4718592 | tf_op jit(solution)/shard_map/all_gather | solution.py:28
  124.1 13.6 %collective-permute-start.13 = (f32[4,4,64,1]{3,1,2,0:T(4,128)S(1)}, f32[4,4,64,1]{3,1,2,0:T(4,128)S(1)}, u32[]{:S(2)}, u32[]{:S(2)}) collective-permute-start(f32[4,4,64,1]{3,1,2,0:T(4,128)S(1)} %get-tuple-element.316), channel_id=1, source_target_pairs={{0,4},{4,8},{8,12},{12,16},{16,20},{20,24},{24,28},{28,0},{1,5},{5... | collective-permute-start | bytes 12296 | tf_op jit(solution)/shard_map/ppermute | solution.py:14
  124.6 13.0 %collective-permute-start.14 = (f32[4,4,64,1]{3,1,2,0:T(4,128)S(1)}, f32[4,4,64,1]{3,1,2,0:T(4,128)S(1)}, u32[]{:S(2)}, u32[]{:S(2)}) collective-permute-start(f32[4,4,64,1]{3,1,2,0:T(4,128)S(1)} %get-tuple-element.317), channel_id=1, source_target_pairs={{4,0},{8,4},{12,8},{16,12},{20,16},{24,20},{28,24},{0,28},{5,1},{9... | collective-permute-start | bytes 12296 | tf_op jit(solution)/shard_map/ppermute | solution.py:15
  137.7 4.0 collective-permute-start.15
  140.8 3.6 collective-permute-start.16
  146.9 14.2 %collective-permute-start.17 = (f32[4,4,64,1]{3,1,2,0:T(4,128)S(1)}, f32[4,4,64,1]{3,1,2,0:T(4,128)S(1)}, u32[]{:S(2)}, u32[]{:S(2)}) collective-permute-start(f32[4,4,64,1]{3,1,2,0:T(4,128)S(1)} %get-tuple-element.314), channel_id=1, source_target_pairs={{0,4},{4,8},{8,12},{12,16},{16,20},{20,24},{24,28},{28,0},{1,5},{5... | collective-permute-start | bytes 12296 | tf_op jit(solution)/shard_map/ppermute | solution.py:14
  146.9 14.1 %collective-permute-start.18 = (f32[4,4,64,1]{3,1,2,0:T(4,128)S(1)}, f32[4,4,64,1]{3,1,2,0:T(4,128)S(1)}, u32[]{:S(2)}, u32[]{:S(2)}) collective-permute-start(f32[4,4,64,1]{3,1,2,0:T(4,128)S(1)} %get-tuple-element.315), channel_id=1, source_target_pairs={{4,0},{8,4},{12,8},{16,12},{20,16},{24,20},{28,24},{0,28},{5,1},{9... | collective-permute-start | bytes 12296 | tf_op jit(solution)/shard_map/ppermute | solution.py:15
  162.5 4.2 collective-permute-start.20
  169.1 14.1 %collective-permute-start.21 = (f32[4,4,64,1]{3,1,2,0:T(4,128)S(1)}, f32[4,4,64,1]{3,1,2,0:T(4,128)S(1)}, u32[]{:S(2)}, u32[]{:S(2)}) collective-permute-start(f32[4,4,64,1]{3,1,2,0:T(4,128)S(1)} %get-tuple-element.312), channel_id=1, source_target_pairs={{0,4},{4,8},{8,12},{12,16},{16,20},{20,24},{24,28},{28,0},{1,5},{5... | collective-permute-start | bytes 12296 | tf_op jit(solution)/shard_map/ppermute | solution.py:14
  169.2 14.0 %collective-permute-start.22 = (f32[4,4,64,1]{3,1,2,0:T(4,128)S(1)}, f32[4,4,64,1]{3,1,2,0:T(4,128)S(1)}, u32[]{:S(2)}, u32[]{:S(2)}) collective-permute-start(f32[4,4,64,1]{3,1,2,0:T(4,128)S(1)} %get-tuple-element.313), channel_id=1, source_target_pairs={{4,0},{8,4},{12,8},{16,12},{20,16},{24,20},{28,24},{0,28},{5,1},{9... | collective-permute-start | bytes 12296 | tf_op jit(solution)/shard_map/ppermute | solution.py:15
  184.8 3.6 collective-permute-start.24
  191.9 15.8 %collective-permute-start.25 = (f32[4,4,64,128]{3,1,2,0:T(4,128)}, f32[4,4,64,128]{3,1,2,0:T(4,128)S(1)}, u32[]{:S(2)}, u32[]{:S(2)}) collective-permute-start(f32[4,4,64,128]{3,1,2,0:T(4,128)} %multiply_add_fusion), channel_id=1, source_target_pairs={{0,32},{32,64},{64,96},{96,128},{128,160},{160,192},{192,224},{1,3... | collective-permute-start | bytes 1572872 | tf_op jit(solution)/shard_map/ppermute | solution.py:23
  (57 other events, 539.3 us)
Sparse Core Ops, SparseCore 0:
  122.3 75.1 all-gather.4
  212.2 76.6 all-gather.6
where the time goes:
time: 476 us; the launch traced here: 468 us
  blocking collectives  149 us (31%)
  waiting for transfers between devices  134 us (28%)
  other arithmetic  66.1 us (14%)
  local copies, waits for them, and re-layouts  50 us (11%)
  starting transfers between devices  41.8 us (9%)
  between operations  23.4 us (5%)
    psum x1, blocking collectives, per_device(): inner, square = lax.psum((local_inner, local_square), ('win', 'tx', 'ty'))  74.7 us
    psum x1, blocking collectives, per_device(): rest_sq = lax.psum(local_rest, ('win', 'tx', 'ty'))  74.1 us
    all_gather x2, waiting for transfers between devices, prefix(): everything = lax.all_gather(value, axis)  73 us
    ppermute x12, waiting for transfers between devices, padded_2(): before = lax.ppermute(last, axis, up)  37.9 us
    ppermute x12, starting transfers between devices, padded_2(): after = lax.ppermute(leading, axis, down)  24.2 us
    select_n x16, other arithmetic, lap(): return jnp.where(reached, new, before)  19.8 us
    slice x9, local copies, waits for them, and re-layouts, padded_2(): last = lax.slice_in_dim(value, length - width, length, axis=dim)  18.1 us
    ppermute x12, waiting for transfers between devices, padded_2(): after = lax.ppermute(leading, axis, down)  14.6 us
  transfers between devices with their start and end apart: 28, of which 19 were waited for; matrix products, arithmetic and copies ran while one was open for 9% of the time, Pallas kernels for 0%

commit v1 on v0

v1 whole, which is shorter than its diff:
```python
import functools
import jax
import jax.numpy as jnp
from jax import lax
from jax.experimental import pallas as pl
from jax.experimental.pallas import tpu as pltpu
from jax.sharding import PartitionSpec as P

VM = pl.BlockSpec(memory_space=pltpu.VMEM)
SM = pl.BlockSpec(memory_space=pltpu.SMEM)
HB = pl.BlockSpec(memory_space=pl.ANY)
NF = 16
NW = 24
NO = 2
ALL = NF + NW + NO + NF
PER = 21
ROWS = 64
EXT = ROWS + 16
LANES = 128


def sds(*shape):
    return jax.ShapeDtypeStruct(shape, jnp.float32)


def lanes_of(i):
    lane = lax.broadcasted_iota(jnp.int32, (8, LANES), 1)
    return (lane >= 6 * i) & (lane < 6 * i + 6)


def pack_fields(fetch, count, first):
    acc = jnp.zeros((8, LANES), jnp.float32)
    for i in range(count):
        acc = jnp.where(lanes_of(i), pltpu.roll(fetch(first + i), (6 * i + 3) % LANES, 1), acc)
    return acc


def edges_kernel(inc, winds, obs, dual, top, bottom, packed):
    parts = ((inc, 0, NF), (winds, NF, NW), (obs, NF + NW, NO), (dual, NF + NW + NO, NF))

    def source(f):
        for ref, start, size in parts:
            if f < start + size:
                return ref, f - start

    for ref, start, size in parts:
        top[start : start + size] = ref[:, 0:8, :]
        bottom[start : start + size] = ref[:, ROWS - 8 : ROWS, :]

    def tile(r, carry):
        rows = pl.ds(pl.multiple_of(r * 8, 8), 8)

        def fetch(f):
            ref, at = source(f)
            return ref[at, rows, :]

        for t in range(3):
            count = min(PER, ALL - t * PER)
            packed[rows, t * LANES : (t + 1) * LANES] = pack_fields(fetch, count, t * PER)
        return carry

    lax.fori_loop(0, ROWS // 8, tile, 0)


def edges_halo_kernel(south, north, packed, full):
    full[8 : 8 + ROWS, :] = packed[...]
    for at, ref in ((0, south), (8 + ROWS, north)):
        for t in range(3):
            count = min(PER, ALL - t * PER)
            full[at : at + 8, t * LANES : (t + 1) * LANES] = pack_fields(
                lambda f: ref[f], count, t * PER
            )


def unpack_columns(strip, i):
    return pltpu.roll(strip, (LANES - 3 - 6 * i) % LANES, 1)


def merged(west, east):
    lane = lax.broadcasted_iota(jnp.int32, west.shape, 1) % 6
    return jnp.where(lane < 3, west, east)


def from_sides(x):
    return pltpu.roll(x, 2 * LANES - 1, 1), pltpu.roll(x, 1, 1)


def rows_shifted(ref, f, r, tiles):
    center = ref[f, 8 * r : 8 * r + 8, :]
    if r == 0:
        south = pltpu.roll(center, 1, 0)
    else:
        south = ref[f, 8 * r - 1 : 8 * r + 7, :]
    if r == tiles - 1:
        north = pltpu.roll(center, 7, 0)
    else:
        north = ref[f, 8 * r + 1 : 8 * r + 9, :]
    return center, north, south


TILES = EXT // 8


def load_winds(winds, south, north, west, east, wind):
    for t in range(2):
        strip = merged(
            west[:, t * LANES : (t + 1) * LANES], east[:, t * LANES : (t + 1) * LANES]
        )
        for i in range(PER):
            f = t * PER + i
            if NF <= f < NF + NW:
                wind[f - NF, :, LANES:] = unpack_columns(strip, i)
    wind[:, 0:8, :LANES] = south[NF : NF + NW]
    wind[:, 8 : 8 + ROWS, :LANES] = winds[...]
    wind[:, 8 + ROWS :, :LANES] = north[NF : NF + NW]


def forward_kernel(
    inc, winds, obs, obsvar, south, north, west, east, diffusion, weight, edge,
    late, pm, wind, xa, xb, oacc,
):
    load_winds(winds, south, north, west, east, wind)
    strip = merged(west[:, :LANES], east[:, :LANES])
    for f in range(NF):
        xa[f, :, LANES:] = unpack_columns(strip, f)
    xa[:, 0:8, :LANES] = south[0:NF]
    xa[:, 8 : 8 + ROWS, :LANES] = inc[...]
    xa[:, 8 + ROWS :, :LANES] = north[0:NF]
    oacc[...] = jnp.zeros_like(oacc)
    keep_south = edge[0]
    keep_north = edge[1]
    bufs = (xa, xb)
    for s in range(3):
        src, dst = bufs[s % 2], bufs[(s + 1) % 2]
        last = s == 2

        def level(l, carry, s=s, src=src, dst=dst, last=last):
            for r in range(1, TILES - 1) if last else range(TILES):
                a = wind[s * 8 + l, 8 * r : 8 * r + 8, :]
                b = wind[s * 8 + 4 + l, 8 * r : 8 * r + 8, :]
                pa, na = jnp.maximum(a, 0.0), jnp.minimum(a, 0.0)
                pb, nb = jnp.maximum(b, 0.0), jnp.minimum(b, 0.0)
                base = 1.0 - (pa - na) - (pb - nb)
                sums = [None] * NO
                for f in range(4):
                    k = diffusion[f, l]
                    center, xn, xs = rows_shifted(src, f * 4 + l, r, TILES)
                    xe, xw = from_sides(center)
                    out = (
                        (base - 4.0 * k) * center
                        + (pa + k) * xw
                        + (k - na) * xe
                        + (pb + k) * xs
                        + (k - nb) * xn
                    )
                    if last:
                        out = out[:, :LANES]
                        late[f * 2 + l // 2, l % 2, 8 * r - 8 : 8 * r, :] = out
                        for o in range(NO):
                            term = weight[o, f * 4 + l] * out
                            sums[o] = term if sums[o] is None else sums[o] + term
                    else:
                        if r == 0:
                            out = out * keep_south
                        if r == TILES - 1:
                            out = out * keep_north
                        dst[f * 4 + l, 8 * r : 8 * r + 8, :] = out
                if last:
                    for o in range(NO):
                        oacc[o, 8 * r - 8 : 8 * r, :] += sums[o]
            return carry

        lax.fori_loop(0, 4, level, 0)
    var = obsvar[...]
    pm[...] = (var * obs[...] + oacc[...]) / var


def adjoint_kernel(
    dual, follow, fhalo, winds, obs, south, north, west, east, diffusion, weight, edge,
    late, wind, ya, yb, ob,
):
    load_winds(winds, south, north, west, east, wind)
    strip1 = merged(west[:, LANES : 2 * LANES], east[:, LANES : 2 * LANES])
    for o in range(NO):
        ob[o, :, LANES:] = unpack_columns(strip1, NF + NW + o - PER)
    ob[:, 0:8, :LANES] = south[NF + NW : NF + NW + NO]
    ob[:, 8 : 8 + ROWS, :LANES] = obs[...]
    ob[:, 8 + ROWS :, :LANES] = north[NF + NW : NF + NW + NO]
    for f in range(NF):
        start = weight[0, f] * ob[0] + weight[1, f] * ob[1]
        ya[f, 0:8, :LANES] = start[0:8, :LANES] - fhalo[f]
        ya[f, 8 : 8 + ROWS, :LANES] = start[8 : 8 + ROWS, :LANES] - follow[f]
        ya[f, 8 + ROWS :, :LANES] = start[8 + ROWS :, :LANES] - fhalo[NF + f]
        for r in range(TILES):
            ya[f, 8 * r : 8 * r + 8, LANES:] = start[
                8 * r : 8 * r + 8, LANES:
            ] - unpack_columns(fhalo[2 * NF + r], f)
    keep_south = edge[0]
    keep_north = edge[1]
    bufs = (ya, yb)
    for step in range(3):
        s = 2 - step
        src, dst = bufs[step % 2], bufs[(step + 1) % 2]
        last = step == 2

        def level(l, carry, s=s, src=src, dst=dst, last=last):
            for r in range(1, TILES - 1) if last else range(TILES):
                a = wind[s * 8 + l, 8 * r : 8 * r + 8, :]
                b, bn, bs = rows_shifted(wind, s * 8 + 4 + l, r, TILES)
                pa, na = jnp.maximum(a, 0.0), jnp.minimum(a, 0.0)
                base = 1.0 - (pa - na) - jnp.abs(b)
                pbn = jnp.maximum(bn, 0.0)
                nbs = jnp.minimum(bs, 0.0)
                for f in range(4):
                    k = diffusion[f, l]
                    center, yn, ys = rows_shifted(src, f * 4 + l, r, TILES)
                    east_of, _ = from_sides((pa + k) * center)
                    _, west_of = from_sides((k - na) * center)
                    out = (
                        (base - 4.0 * k) * center
                        + east_of
                        + west_of
                        + (pbn + k) * yn
                        + (k - nbs) * ys
                    )
                    if last:
                        rows = slice(8 * r - 8, 8 * r)
                        late[f * 2 + l // 2, l % 2, rows, :] = (
                            out[:, :LANES] + dual[f * 4 + l, rows, :]
                        )
                    else:
                        if r == 0:
                            out = out * keep_south
                        if r == TILES - 1:
                            out = out * keep_north
                        dst[f * 4 + l, 8 * r : 8 * r + 8, :] = out
            return carry

        lax.fori_loop(0, 4, level, 0)


def scan_kernel(windows, late, early, pm, obs, back, totals, wv, vv, rr):
    wv[...] = jnp.zeros_like(wv)
    vv[...] = jnp.zeros_like(vv)

    def tile(r, carry):
        rows = pl.ds(pl.multiple_of(r * 8, 8), 8)
        for c in range(2):
            run = jnp.zeros((8, LANES), jnp.float32)
            inner = jnp.zeros((8, LANES), jnp.float32)
            square = jnp.zeros((8, LANES), jnp.float32)
            sums = [None] * windows
            for v in reversed(range(windows)):
                run = run + late[v, 2 + c, rows, :]
                sums[v] = run
                back[v, c, rows, :] = run
            run = jnp.zeros((8, LANES), jnp.float32)
            for v in range(windows):
                lam = early[v, c, rows, :]
                inc = early[v, 2 + c, rows, :]
                var = early[v, 4 + c, rows, :]
                term = var * (lam - sums[v]) + inc
                if v:
                    term = term - late[v - 1, c, rows, :]
                run = run + term
                back[v, 2 + c, rows, :] = run
                inner = inner + sums[v] * lam + run * inc
                square = square + lam * lam + inc * inc
            wv[...] += inner
            vv[...] += square
        return carry

    lax.fori_loop(0, ROWS // 8, tile, 0)
    for o in range(NO):
        for r in range(ROWS // 8):
            rows = slice(8 * r, 8 * r + 8)
            x = obs[o, rows, :]
            wv[...] += pm[o, rows, :] * x
            vv[...] += x * x
    inner = jnp.sum(wv[...], keepdims=True)
    square = jnp.sum(vv[...], keepdims=True)
    h = jnp.where(square > 0.0, inner / jnp.where(square > 0.0, square, 1.0), 0.0)
    rr[...] = jnp.zeros_like(rr)

    def rest(r, carry):
        rows = pl.ds(pl.multiple_of(r * 8, 8), 8)
        acc = jnp.zeros((8, LANES), jnp.float32)
        for v in range(windows):
            for c in range(4):
                d = back[v, c, rows, :] - h * early[v, c, rows, :]
                acc = acc + d * d
        for o in range(NO):
            d = pm[o, rows, :] - h * obs[o, rows, :]
            acc = acc + d * d
        rr[...] += acc
        return carry

    lax.fori_loop(0, ROWS // 8, rest, 0)
    remain = jnp.sum(rr[...], keepdims=True)
    lane = lax.broadcasted_iota(jnp.int32, totals.shape, 1)
    totals[...] = jnp.where(
        lane == 0, inner, jnp.where(lane == 1, square, jnp.where(lane == 2, remain, 0.0))
    )


def final_kernel(count, totals, back, dual, inc, pm, obs, o_dual, o_obs, o_inc, coeffs):
    t = totals[...]
    lane = lax.broadcasted_iota(jnp.int32, t.shape, 1)
    inner = jnp.where(lane == 0, t, 0.0)
    square = jnp.where(lane == 0, pltpu.roll(t, LANES - 1, 1), 0.0)
    remain = jnp.where(lane == 0, pltpu.roll(t, LANES - 2, 1), 0.0)
    h_own = jnp.where(square > 0.0, inner / jnp.where(square > 0.0, square, 1.0), 0.0)
    h = jnp.sum(inner, keepdims=True) / jnp.sum(square, keepdims=True)
    d = h - h_own
    uu = jnp.sum(remain + square * d * d, keepdims=True)
    scale = jnp.sqrt(uu / count + 1e-06)
    inv = 1.0 / scale
    first = (lax.broadcasted_iota(jnp.int32, (8, LANES), 0) == 0) & (
        lax.broadcasted_iota(jnp.int32, (8, LANES), 1) == 0
    )
    coeffs[0] = jnp.sum(jnp.where(first, h, 0.0))
    coeffs[1] = jnp.sum(jnp.where(first, scale, 0.0))
    for f in range(NF):
        o_dual[f] = (back[f // 2, f % 2] - h * dual[f]) * inv
        o_inc[f] = (back[f // 2, 2 + f % 2] - h * inc[f]) * inv
    o_obs[...] = (pm[...] - h * obs[...]) * inv


def per_device(dual, obs_dual, increment, trajectory, diffusion, obs_weight, model_var, obs_var):
    windows = lax.axis_size("win")
    columns = lax.axis_size("tx")
    ranks = lax.axis_size("ty")
    lam = dual.reshape(NF, ROWS, LANES)
    inc = increment.reshape(NF, ROWS, LANES)
    winds = trajectory.reshape(NW, ROWS, LANES)
    obs = obs_dual.reshape(NO, ROWS, LANES)
    var = model_var.reshape(NF, ROWS, LANES)
    obsvar = obs_var.reshape(NO, ROWS, LANES)
    weight = obs_weight.reshape(NO, NF)
    row = lax.axis_index("ty")
    edge = jnp.stack([row > 0, row < ranks - 1]).astype(jnp.float32)
    to_previous = [(i + 1, i) for i in range(windows - 1)]

    follow = lax.ppermute(lam, "win", to_previous)
    top, bottom, packed = pl.pallas_call(
        edges_kernel,
        out_shape=(sds(ALL, 8, LANES), sds(ALL, 8, LANES), sds(ROWS, 3 * LANES)),
        in_specs=[VM] * 4,
        out_specs=(VM, VM, VM),
        name="edges",
    )(inc, winds, obs, lam)
    south = lax.ppermute(bottom, "ty", [(i, i + 1) for i in range(ranks - 1)])
    north = lax.ppermute(top, "ty", [(i + 1, i) for i in range(ranks - 1)])
    full = pl.pallas_call(
        edges_halo_kernel,
        out_shape=sds(EXT, 3 * LANES),
        in_specs=[VM] * 3,
        out_specs=VM,
        name="edges_halo",
    )(south, north, packed)
    west = lax.ppermute(full, "tx", [(i, (i + 1) % columns) for i in range(columns)])
    east = lax.ppermute(full, "tx", [((i + 1) % columns, i) for i in range(columns)])

    early = jnp.concatenate(
        [x.reshape(windows, NF // windows, ROWS, LANES) for x in (lam, inc, var)], axis=1
    )
    early = lax.all_to_all(early, "win", 0, 0)

    strip = merged(west[:, 2 * LANES :], east[:, 2 * LANES :])
    fhalo = jnp.concatenate(
        [south[ALL - NF :], north[ALL - NF :], strip.reshape(TILES, 8, LANES)], axis=0
    )
    fhalo = lax.ppermute(fhalo, "win", to_previous)

    field = pltpu.VMEM((NF, EXT, 2 * LANES), jnp.float32)
    wind = pltpu.VMEM((NW, EXT, 2 * LANES), jnp.float32)
    moved, pm = pl.pallas_call(
        forward_kernel,
        out_shape=(sds(windows, NF // windows, ROWS, LANES), sds(NO, ROWS, LANES)),
        in_specs=[VM] * 8 + [SM] * 3,
        out_specs=(VM, VM),
        scratch_shapes=[wind, field, field, pltpu.VMEM((NO, ROWS, LANES), jnp.float32)],
        name="forward",
    )(inc, winds, obs, obsvar, south, north, west, east, diffusion, weight, edge)
    zd = pl.pallas_call(
        adjoint_kernel,
        out_shape=sds(windows, NF // windows, ROWS, LANES),
        in_specs=[VM] * 9 + [SM] * 3,
        out_specs=VM,
        scratch_shapes=[wind, field, field, pltpu.VMEM((NO, EXT, 2 * LANES), jnp.float32)],
        name="adjoint",
    )(lam, follow, fhalo, winds, obs, south, north, west, east, diffusion, weight, edge)

    late = lax.all_to_all(jnp.concatenate([moved, zd], axis=1), "win", 0, 0)
    devices = windows * columns * ranks
    tile = pltpu.VMEM((8, LANES), jnp.float32)
    back, totals = pl.pallas_call(
        functools.partial(scan_kernel, windows),
        out_shape=(sds(windows, 4, ROWS, LANES), sds(devices, LANES)),
        in_specs=[VM] * 4,
        out_specs=(VM, VM),
        scratch_shapes=[tile, tile, tile],
        name="scans",
    )(late, early, pm, obs)
    totals = lax.all_to_all(totals, ("win", "tx", "ty"), 0, 0)
    back = lax.all_to_all(back, "win", 0, 0)

    count = float((2 * NF + NO) * ROWS * LANES * devices)
    o_dual, o_obs, o_inc, coeffs = pl.pallas_call(
        functools.partial(final_kernel, count),
        out_shape=(sds(NF, ROWS, LANES), sds(NO, ROWS, LANES), sds(NF, ROWS, LANES), sds(2)),
        in_specs=[VM] * 6,
        out_specs=(VM, VM, VM, SM),
        name="final",
    )(totals, back, lam, inc, pm, obs)
    return (
        o_dual.reshape(dual.shape),
        o_obs.reshape(obs_dual.shape),
        o_inc.reshape(increment.shape),
        coeffs,
    )


def solution(mesh):
    in_specs = (
        P("win", None, None, "ty", "tx"),
        P("win", None, "ty", "tx"),
        P("win", None, None, "ty", "tx"),
        P("win", None, None, None, "ty", "tx"),
        P(),
        P(),
        P("win", None, None, "ty", "tx"),
        P("win", None, "ty", "tx"),
    )
    out_specs = (
        P("win", None, None, "ty", "tx"),
        P("win", None, "ty", "tx"),
        P("win", None, None, "ty", "tx"),
        P(),
    )
    return jax.shard_map(
        per_device, mesh=mesh, in_specs=in_specs, out_specs=out_specs, check_vma=False
    )
```

time: 476 us -> 132 us (0.28); the launches traced: 468 us -> 131 us
  waiting for transfers between devices: 134 us -> 15 us
  blocking collectives: 149 us -> 61 us
  other arithmetic: 66.1 us -> 4.47 us
  local copies, waits for them, and re-layouts: 50 us -> 4.5 us
  Pallas kernels: 0 us -> 24.4 us
  between operations: 23.4 us -> 0.77 us
  starting transfers between devices: 41.8 us -> 20.6 us
    psum x2 -> x0, blocking collectives: 149 us -> none  [the longest x1 74.7 us: per_device(): inner, square = lax.psum((local_inner, local_square), ('win', 'tx', 'ty'))]
    all_gather x2 -> x0, waiting for transfers between devices: 73 us -> none  [prefix(): everything = lax.all_gather(value, axis)]
    all_to_all x0 -> x3, blocking collectives: none -> 61 us  [the longest x1 22.3 us: per_device(): late = lax.all_to_all(jnp.concatenate([moved, zd], axis=1), 'win', 0, 0)]
    ppermute x26 -> x6, waiting for transfers between devices: 61.3 us -> 15 us  [the longest x1 10.6 us: per_device(): south = lax.ppermute(bottom, 'ty', [(i, i + 1) for i in range(ranks - 1)])]
    ppermute x26 -> x6, starting transfers between devices: 41.8 us -> 13.1 us  [the longest x1 5.58 us: per_device(): lax.ppermute(full, 'tx', [((i + 1) % columns, i) for i in range(columns)])]
    pallas_call x0 -> x6, Pallas kernels: none -> 24.4 us  [the longest x1 6.48 us: per_device(): pl.pallas_call(adjoint_kernel, out_shape=sds(windows, NF // windows, ROWS...]
    slice x12 -> x2, local copies, waits for them, and re-layouts: 25.4 us -> 1.69 us  [the longest x1 0.84 us: per_device(): south[ALL - NF:]]
    select_n x17 -> x0, other arithmetic: 19.8 us -> none  [the longest x16 19.8 us: lap(): return jnp.where(reached, new, before)]
  transfers between devices with their start and end apart: 28 -> 7, of which waited for: 19 -> 4; matrix products, arithmetic and copies ran while one was open for 9% -> 3% of each run, Pallas kernels for 0% -> 14%
where the time goes in v1:
time: 132 us; the launch traced here: 131 us
  blocking collectives  61 us (46%)
  Pallas kernels  24.4 us (18%)
  starting transfers between devices  20.6 us (16%)
  waiting for transfers between devices  15 us (11%)
  local copies, waits for them, and re-layouts  4.5 us (3%)
  other arithmetic  4.47 us (3%)
    all_to_all x1, blocking collectives, per_device(): late = lax.all_to_all(jnp.concatenate([moved, zd], axis=1), 'win', 0, 0)  22.3 us
    all_to_all x1, blocking collectives, per_device(): back = lax.all_to_all(back, 'win', 0, 0)  19.7 us
    all_to_all x1, blocking collectives, per_device(): totals = lax.all_to_all(totals, ('win', 'tx', 'ty'), 0, 0)  18.9 us
    ppermute x1, waiting for transfers between devices, per_device(): south = lax.ppermute(bottom, 'ty', [(i, i + 1) for i in range(ranks - 1)])  10.6 us
    all_to_all x1, starting transfers between devices, per_device(): early = lax.all_to_all(early, 'win', 0, 0)  7.47 us
    pallas_call x1, Pallas kernels, per_device(): pl.pallas_call(adjoint_kernel, out_shape=sds(windows, NF // windows, ROWS...  6.48 us
    pallas_call x1, Pallas kernels, per_device(): pl.pallas_call(forward_kernel, out_shape=(sds(windows, NF // windows, ROW...  5.91 us
    ppermute x1, starting transfers between devices, per_device(): lax.ppermute(full, 'tx', [((i + 1) % columns, i) for i in range(columns)])  5.58 us
  transfers between devices with their start and end apart: 7, of which 4 were waited for; matrix products, arithmetic and copies ran while one was open for 3% of the time, Pallas kernels for 14%

profile of v1, /device:TPU:1, one launch (start us, length us, event | category | flops | bytes accessed | tf_op | source)
XLA Modules:
  0.0 130.7 jit_solution(15553082195904224933)
XLA Ops:
  0.6 2.7 %pad_maximum_fusion = f32[8,6,64,128]{3,2,1,0:T(8,128)} fusion(f32[8,2,64,128]{3,2,1,0:T(8,128)} %bitcast.37, f32[8,2,64,128]{3,2,1,0:T(8,128)} %bitcast.19, f32[8,2,64,128]{3,2,1,0:T(8,128)} %bitcast.23), kind=kLoop, calls=%fused_computation | loop fusion | flops 786432 | bytes 3145728 | tf_op jit(solution)/shard_map/concatenate | solution.py:364
  3.3 7.5 %all-to-all-start.1 = ((f32[8,6,64,128]{3,2,1,0:T(8,128)}), f32[8,6,64,128]{3,2,1,0:T(8,128)S(1)}, u32[]{:S(2)}, u32[]{:S(2)}) async-start(f32[8,6,64,128]{3,2,1,0:T(8,128)} %pad_maximum_fusion), calls=%async_computation.1 | async-start | bytes 3145728 | tf_op jit(solution)/shard_map/all_to_all | solution.py:367
  10.8 3.3 %edges.1 = (f32[58,8,128]{2,1,0:T(8,128)}, f32[58,8,128]{2,1,0:T(8,128)}, f32[64,384]{1,0:T(8,128)}) custom-call(f32[16,64,128]{2,1,0:T(8,128)} %bitcast.20, f32[24,64,128]{2,1,0:T(8,128)} %bitcast.28, f32[2,64,128]{2,1,0:T(8,128)} %bitcast.31, f32[16,64,128]{2,1,0:T(8,128)} %bitcast.24), custom_call_target="tpu_custom_call" | custom-call | tf_op jit(solution)/shard_map/edges/pallas_call | solution.py:345
  14.1 3.0 %collective-permute-start = (f32[58,8,128]{2,1,0:T(8,128)}, f32[58,8,128]{2,1,0:T(8,128)S(1)}, u32[]{:S(2)}, u32[]{:S(2)}) collective-permute-start(f32[58,8,128]{2,1,0:T(8,128)} %get-tuple-element.15), channel_id=1, source_target_pairs={{0,1},{1,2},{2,3},{4,5},{5,6},{6,7},{8,9},{9,10},{10,11},{12,13},{... | collective-permute-start | bytes 712712 | tf_op jit(solution)/shard_map/ppermute | solution.py:352
  17.2 1.9 %collective-permute-start.1 = (f32[58,8,128]{2,1,0:T(8,128)}, f32[58,8,128]{2,1,0:T(8,128)S(1)}, u32[]{:S(2)}, u32[]{:S(2)}) collective-permute-start(f32[58,8,128]{2,1,0:T(8,128)} %get-tuple-element.16), channel_id=1, source_target_pairs={{1,0},{2,1},{3,2},{5,4},{6,5},{7,6},{9,8},{10,9},{11,10},{13,12},{... | collective-permute-start | bytes 712712 | tf_op jit(solution)/shard_map/ppermute | solution.py:353
  19.1 1.3 collective-permute-start.4
  20.4 10.6 %collective-permute-done.south = f32[58,8,128]{2,1,0:T(8,128)S(1)} collective-permute-done((f32[58,8,128]{2,1,0:T(8,128)}, f32[58,8,128]{2,1,0:T(8,128)S(1)}, u32[]{:S(2)}, u32[]{:S(2)}) %collective-permute-start) | collective-permute-done | bytes 237600 | tf_op jit(solution)/shard_map/ppermute | solution.py:352
  31.1 0.9 collective-permute-done.1.north
  32.7 2.0 %edges_halo.1 = f32[80,384]{1,0:T(8,128)} custom-call(f32[58,8,128]{2,1,0:T(8,128)} %copy-done.2, f32[58,8,128]{2,1,0:T(8,128)} %copy-done.3, f32[64,384]{1,0:T(8,128)} %get-tuple-element.17.packed), custom_call_target="tpu_custom_call" | custom-call | tf_op jit(solution)/shard_map/edges_halo/pallas_call | solution.py:354
  34.6 5.6 %collective-permute-start.3 = (f32[80,384]{1,0:T(8,128)}, f32[80,384]{1,0:T(8,128)S(1)}, u32[]{:S(2)}, u32[]{:S(2)}) collective-permute-start(f32[80,384]{1,0:T(8,128)} %edges_halo.1), channel_id=1, source_target_pairs={{4,0},{8,4},{12,8},{16,12},{20,16},{24,20},{28,24},{0,28},{5,1},{9... | collective-permute-start | bytes 368648 | tf_op jit(solution)/shard_map/ppermute | solution.py:362
  40.2 0.8 slice.16
  41.1 0.8 slice.17
  42.4 3.0 %collective-permute-done.2.west = f32[80,384]{1,0:T(8,128)S(1)} collective-permute-done((f32[80,384]{1,0:T(8,128)}, f32[80,384]{1,0:T(8,128)S(1)}, u32[]{:S(2)}, u32[]{:S(2)}) %collective-permute-start.2) | collective-permute-done | bytes 122912 | tf_op jit(solution)/shard_map/ppermute | solution.py:361
  45.4 1.3 collective-permute-start.5
  47.9 5.9 %forward.1 = (f32[8,2,64,128]{3,2,1,0:T(8,128)}, f32[2,64,128]{2,1,0:T(8,128)}) custom-call(f32[16,64,128]{2,1,0:T(8,128)} %bitcast.21, f32[24,64,128]{2,1,0:T(8,128)} %bitcast.29, f32[2,64,128]{2,1,0:T(8,128)} %bitcast.32, f32[2,64,128]{2,1,0:T(8,128)} %bitcast.39, f32[58,8,128]{2,1,0:T(8,128)} %copy-done.2, f32[58,8,128]{2,1,0:T(8,128)} %copy-done.3, ...), custom_call_target="tpu_custom_call" | custom-call | tf_op jit(solution)/shard_map/forward/pallas_call | solution.py:377
  53.9 0.8 copy-done.6
  54.6 0.7 copy-done.8
  55.3 6.5 %adjoint.1 = f32[8,2,64,128]{3,2,1,0:T(8,128)} custom-call(f32[16,64,128]{2,1,0:T(8,128)} %bitcast.25, f32[16,64,128]{2,1,0:T(8,128)} %copy-done.6, f32[42,8,128]{2,1,0:T(8,128)} %copy-done.8, f32[24,64,128]{2,1,0:T(8,128)} %bitcast.30, f32[2,64,128]{2,1,0:T(8,128)} %bitcast.33, f32[58,8,128]{2,1,0:T(8,128)} %copy-done.2, f32[58,8,128]{2,1,0:T(8,128)} %copy-done.3, ...), custom_call_target="tpu_custom_call" | custom-call | tf_op jit(solution)/shard_map/adjoint/pallas_call | solution.py:385
  61.8 1.1 pad_maximum_fusion.1
  63.0 22.3 %all_to_all.26.late = f32[8,4,64,128]{3,2,1,0:T(8,128)} all-to-all(f32[8,4,64,128]{3,2,1,0:T(8,128)S(1)} %pad_maximum_fusion.1), channel_id=1, replica_groups=mesh['win'=8,'tx'=8,'ty'=4] {'win'}, dimensions={0} | all-to-all | bytes 2097152 | tf_op jit(solution)/shard_map/all_to_all | solution.py:394
  85.3 3.7 %scans.1 = (f32[8,4,64,128]{3,2,1,0:T(8,128)}, f32[256,128]{1,0:T(8,128)}) custom-call(f32[8,4,64,128]{3,2,1,0:T(8,128)} %all_to_all.26.late, f32[8,6,64,128]{3,2,1,0:T(8,128)} %copy-done.1, f32[2,64,128]{2,1,0:T(8,128)} %get-tuple-element.19.pm, f32[2,64,128]{2,1,0:T(8,128)} %bitcast.34), custom_call_target="tpu_custom_call" | custom-call | tf_op jit(solution)/shard_map/scans/pallas_call | solution.py:397
  89.0 18.9 %all_to_all.27 = f32[256,1,128]{2,1,0:T(1,128)} all-to-all(f32[256,1,128]{2,1,0:T(1,128)} %bitcast.38), channel_id=1, replica_groups=mesh['win'=8,'tx'=8,'ty'=4] {'win','tx','ty'}, dimensions={0} | all-to-all | bytes 262144 | tf_op jit(solution)/shard_map/all_to_all | solution.py:405
  107.9 19.7 %all_to_all.28.back = f32[8,4,64,128]{3,2,1,0:T(8,128)} all-to-all(f32[8,4,64,128]{3,2,1,0:T(8,128)} %get-tuple-element.21), channel_id=1, replica_groups=mesh['win'=8,'tx'=8,'ty'=4] {'win'}, dimensions={0} | all-to-all | bytes 2097152 | tf_op jit(solution)/shard_map/all_to_all | solution.py:406
  127.7 3.0 %final.1 = (f32[16,64,128]{2,1,0:T(8,128)}, f32[2,64,128]{2,1,0:T(8,128)}, f32[16,64,128]{2,1,0:T(8,128)}, f32[2]{0:T(128)}) custom-call(f32[256,128]{1,0:T(8,128)} %bitcast.36, f32[8,4,64,128]{3,2,1,0:T(8,128)} %all_to_all.28.back, f32[16,64,128]{2,1,0:T(8,128)} %bitcast.26, f32[16,64,128]{2,1,0:T(8,128)} %bitcast.22, f32[2,64,128]{2,1,0:T(8,128)} %get-tuple-element.19.pm, ...), custom_call_target="tpu_custom_call" | custom-call | tf_op jit(solution)/shard_map/final/pallas_call | solution.py:409
  (29 shorter events, 2.5 us)
Async XLA Ops:
  3.3 59.6 %all-to-all-start.1 = ((f32[8,6,64,128]{3,2,1,0:T(8,128)}), f32[8,6,64,128]{3,2,1,0:T(8,128)S(1)}, u32[]{:S(2)}, u32[]{:S(2)}) async-start(f32[8,6,64,128]{3,2,1,0:T(8,128)} %pad_maximum_fusion), calls=%async_computation.1 | async-start | bytes 3145728 | tf_op jit(solution)/shard_map/all_to_all | solution.py:367
  10.8 8.3 %copy-start = (f32[1,4,4,64,128]{4,3,2,1,0:T(8,128)S(1)}, f32[1,4,4,64,128]{4,3,2,1,0:T(8,128)}, u32[]{:S(2)}) copy-start(f32[1,4,4,64,128]{4,3,2,1,0:T(8,128)} %param.8) | copy-start | bytes 1572868
  10.8 35.9 %copy-start.9 = (f32[2,4,4]{2,1,0:T(4,128)S(1)}, f32[2,4,4]{2,1,0:T(4,128)}, u32[]{:S(2)}) copy-start(f32[2,4,4]{2,1,0:T(4,128)} %param.13) | copy-start | bytes 388
  14.1 16.9 %collective-permute-start = (f32[58,8,128]{2,1,0:T(8,128)}, f32[58,8,128]{2,1,0:T(8,128)S(1)}, u32[]{:S(2)}, u32[]{:S(2)}) collective-permute-start(f32[58,8,128]{2,1,0:T(8,128)} %get-tuple-element.15), channel_id=1, source_target_pairs={{0,1},{1,2},{2,3},{4,5},{5,6},{6,7},{8,9},{9,10},{10,11},{12,13},{... | collective-permute-start | bytes 712712 | tf_op jit(solution)/shard_map/ppermute | solution.py:352
  17.2 14.8 %collective-permute-start.1 = (f32[58,8,128]{2,1,0:T(8,128)}, f32[58,8,128]{2,1,0:T(8,128)S(1)}, u32[]{:S(2)}, u32[]{:S(2)}) collective-permute-start(f32[58,8,128]{2,1,0:T(8,128)} %get-tuple-element.16), channel_id=1, source_target_pairs={{1,0},{2,1},{3,2},{5,4},{6,5},{7,6},{9,8},{10,9},{11,10},{13,12},{... | collective-permute-start | bytes 712712 | tf_op jit(solution)/shard_map/ppermute | solution.py:353
  19.1 34.7 %collective-permute-start.4 = (f32[16,64,128]{2,1,0:T(8,128)S(1)}, f32[16,64,128]{2,1,0:T(8,128)S(1)}, u32[]{:S(2)}, u32[]{:S(2)}) collective-permute-start(f32[16,64,128]{2,1,0:T(8,128)S(1)} %bitcast.27), channel_id=1, source_target_pairs={{32,0},{64,32},{96,64},{128,96},{160,128},{192,160},{224,192},{33,... | collective-permute-start | bytes 1572872 | tf_op jit(solution)/shard_map/ppermute | solution.py:344
  31.1 0.9 copy-start.2
  32.0 0.7 copy-start.3
  34.6 7.8 %collective-permute-start.3 = (f32[80,384]{1,0:T(8,128)}, f32[80,384]{1,0:T(8,128)S(1)}, u32[]{:S(2)}, u32[]{:S(2)}) collective-permute-start(f32[80,384]{1,0:T(8,128)} %edges_halo.1), channel_id=1, source_target_pairs={{4,0},{8,4},{12,8},{16,12},{20,16},{24,20},{28,24},{0,28},{5,1},{9... | collective-permute-start | bytes 368648 | tf_op jit(solution)/shard_map/ppermute | solution.py:362
  40.2 5.2 %collective-permute-start.2 = (f32[80,384]{1,0:T(8,128)}, f32[80,384]{1,0:T(8,128)S(1)}, u32[]{:S(2)}, u32[]{:S(2)}) collective-permute-start(f32[80,384]{1,0:T(8,128)} %edges_halo.1), channel_id=1, source_target_pairs={{0,4},{4,8},{8,12},{12,16},{16,20},{20,24},{24,28},{28,0},{1,5},{5... | collective-permute-start | bytes 368648 | tf_op jit(solution)/shard_map/ppermute | solution.py:361
  42.4 5.6 %copy-start.4 = (f32[80,384]{1,0:T(8,128)}, f32[80,384]{1,0:T(8,128)S(1)}, u32[]{:S(2)}) copy-start(f32[80,384]{1,0:T(8,128)S(1)} %collective-permute-done.3.east) | copy-start | bytes 368644
  45.3 2.6 %copy-start.5 = (f32[80,384]{1,0:T(8,128)}, f32[80,384]{1,0:T(8,128)S(1)}, u32[]{:S(2)}) copy-start(f32[80,384]{1,0:T(8,128)S(1)} %collective-permute-done.2.west) | copy-start | bytes 368644
  45.4 8.5 %collective-permute-start.5 = (f32[42,8,128]{2,1,0:T(8,128)S(1)}, f32[42,8,128]{2,1,0:T(8,128)S(1)}, u32[]{:S(2)}, u32[]{:S(2)}) collective-permute-start(f32[42,8,128]{2,1,0:T(8,128)S(1)} %pad_maximum_fusion.2), channel_id=1, source_target_pairs={{32,0},{64,32},{96,64},{128,96},{160,128},{192,160},{224,192},{33,... | collective-permute-start | bytes 516104 | tf_op jit(solution)/shard_map/ppermute | solution.py:373
  53.8 0.8 copy-start.6
  53.9 8.0 %copy-start.7 = (f32[8,2,64,128]{3,2,1,0:T(8,128)S(1)}, f32[8,2,64,128]{3,2,1,0:T(8,128)}, u32[]{:S(2)}) copy-start(f32[8,2,64,128]{3,2,1,0:T(8,128)} %get-tuple-element.18) | copy-start | bytes 1572868
  54.6 0.7 copy-start.8
  63.0 22.3 %copy-start.1 = (f32[8,6,64,128]{3,2,1,0:T(8,128)}, f32[8,6,64,128]{3,2,1,0:T(8,128)S(1)}, u32[]{:S(2)}) copy-start(f32[8,6,64,128]{3,2,1,0:T(8,128)S(1)} %all-to-all-done.1.early) | copy-start | bytes 4718596

commit v2 on v1

v2 whole, which is shorter than its diff:
```python
import functools
import jax
import jax.numpy as jnp
from jax import lax
from jax.experimental import pallas as pl
from jax.experimental.pallas import tpu as pltpu
from jax.sharding import PartitionSpec as P

VM = pl.BlockSpec(memory_space=pltpu.VMEM)
SM = pl.BlockSpec(memory_space=pltpu.SMEM)
HB = pl.BlockSpec(memory_space=pl.ANY)
NF = 16
NW = 24
NO = 2
ALL = NF + NF + NW + NO
D0, X0, W0, O0 = 0, NF, 2 * NF, 2 * NF + NW
PER = 21
GROUPS = ((D0, NF), (X0, PER), (X0 + PER, PER))
ROWS = 64
EXT = ROWS + 16
LANES = 128
GRANT = pltpu.CompilerParams(vmem_limit_bytes=16 * 1024 * 1024)


def sds(*shape):
    return jax.ShapeDtypeStruct(shape, jnp.float32)


def vmem(*shape):
    return pltpu.VMEM(shape, jnp.float32)


def far(x):
    return pltpu.with_memory_space_constraint(x, pltpu.HBM)


def held(x):
    return pltpu.with_memory_space_constraint(x, pltpu.VMEM)


def lanes_of(i):
    lane = lax.broadcasted_iota(jnp.int32, (8, LANES), 1)
    return (lane >= 6 * i) & (lane < 6 * i + 6)


def pack_fields(fetch, count, first):
    acc = jnp.zeros((8, LANES), jnp.float32)
    for i in range(count):
        acc = jnp.where(lanes_of(i), pltpu.roll(fetch(first + i), (6 * i + 3) % LANES, 1), acc)
    return acc


def edges_kernel(*refs):
    tops, bottoms, (top, bottom) = refs[0:4], refs[4:8], refs[8:]
    start = 0
    for a, b in zip(tops, bottoms):
        size = a.shape[0]
        top[start : start + size] = a[...]
        bottom[start : start + size] = b[...]
        start += size
    top[0, 7:8, :] = jnp.ones((1, LANES), jnp.float32)
    bottom[0, 0:1, :] = jnp.ones((1, LANES), jnp.float32)


def pack_kernel(dual, inc, winds, obs, packed):
    parts = ((dual, D0, NF), (inc, X0, NF), (winds, W0, NW), (obs, O0, NO))

    def tile(r, carry):
        rows = pl.ds(pl.multiple_of(r * 8, 8), 8)

        def fetch(f):
            for ref, start, size in parts:
                if f < start + size:
                    return ref[f - start, rows, :]

        for t, (first, count) in enumerate(GROUPS):
            packed[rows, t * LANES : (t + 1) * LANES] = pack_fields(fetch, count, first)
        return carry

    lax.fori_loop(0, ROWS // 8, tile, 0)


def edges_halo_kernel(south, north, packed, full):
    full[8 : 8 + ROWS, :] = packed[...]
    for at, ref in ((0, south), (8 + ROWS, north)):
        for t, (first, count) in enumerate(GROUPS):
            full[at : at + 8, t * LANES : (t + 1) * LANES] = pack_fields(
                lambda f: ref[f], count, first
            )


def follow_halo_kernel(south, north, west, east, out):
    out[0:NF] = south[0:NF]
    out[NF : 2 * NF] = north[0:NF]
    for r in range(TILES):
        rows = slice(8 * r, 8 * r + 8)
        out[2 * NF + r] = merged(west[rows, 0:LANES], east[rows, 0:LANES])


def unpack_columns(strip, i):
    return pltpu.roll(strip, (LANES - 3 - 6 * i) % LANES, 1)


def merged(west, east):
    lane = lax.broadcasted_iota(jnp.int32, west.shape, 1) % 6
    return jnp.where(lane < 3, west, east)


def from_sides(x):
    return pltpu.roll(x, 2 * LANES - 1, 1), pltpu.roll(x, 1, 1)


def rows_shifted(ref, f, r, tiles):
    center = ref[f, 8 * r : 8 * r + 8, :]
    if r == 0:
        south = pltpu.roll(center, 1, 0)
    else:
        south = ref[f, 8 * r - 1 : 8 * r + 7, :]
    if r == tiles - 1:
        north = pltpu.roll(center, 7, 0)
    else:
        north = ref[f, 8 * r + 1 : 8 * r + 9, :]
    return center, north, south


TILES = EXT // 8


def strip_of(west, east, t):
    lanes = slice((t + 1) * LANES, (t + 2) * LANES)
    return merged(west[:, lanes], east[:, lanes])


def load_field(ref, at, f, rows, south, north, strips):
    ref[at, 0:8, :LANES] = south[f]
    ref[at, 8 : 8 + ROWS, :LANES] = rows
    ref[at, 8 + ROWS :, :LANES] = north[f]
    place = f - X0
    ref[at, :, LANES:] = unpack_columns(strips[place // PER], place % PER)


def load_winds(winds, south, north, strips, wind):
    for i in range(NW):
        load_field(wind, i, W0 + i, winds[i], south, north, strips)


def forward_kernel(
    inc, dual, var, winds, obs, obsvar, south, north, west, east, diffusion, weight,
    late, moved, pm, wind, xa, xb, oacc,
):
    strips = [strip_of(west, east, t) for t in range(2)]
    load_winds(winds, south, north, strips, wind)
    for f in range(NF):
        load_field(xa, f, X0 + f, inc[f], south, north, strips)
    oacc[...] = jnp.zeros_like(oacc)
    keep_south = south[D0, 0:1, 0:1]
    keep_north = north[D0, 7:8, 0:1]
    bufs = (xa, xb)
    for s in range(3):
        src, dst = bufs[s % 2], bufs[(s + 1) % 2]
        last = s == 2

        def level(l, carry, s=s, src=src, dst=dst, last=last):
            for r in range(1, TILES - 1) if last else range(TILES):
                a = wind[s * 8 + l, 8 * r : 8 * r + 8, :]
                b = wind[s * 8 + 4 + l, 8 * r : 8 * r + 8, :]
                pa, na = jnp.maximum(a, 0.0), jnp.minimum(a, 0.0)
                pb, nb = jnp.maximum(b, 0.0), jnp.minimum(b, 0.0)
                base = 1.0 - (pa - na) - (pb - nb)
                sums = [None] * NO
                for f in range(4):
                    k = diffusion[f, l]
                    center, xn, xs = rows_shifted(src, f * 4 + l, r, TILES)
                    xe, xw = from_sides(center)
                    out = (
                        (base - 4.0 * k) * center
                        + (pa + k) * xw
                        + (k - na) * xe
                        + (pb + k) * xs
                        + (k - nb) * xn
                    )
                    if last:
                        out = out[:, :LANES]
                        n = f * 4 + l
                        rows = slice(8 * r - 8, 8 * r)
                        moved[n, rows, :] = out
                        late[f * 2 + l // 2, l % 2, rows, :] = (
                            var[n, rows, :] * dual[n, rows, :] + inc[n, rows, :] - out
                        )
                        for o in range(NO):
                            term = weight[o, f, l] * out
                            sums[o] = term if sums[o] is None else sums[o] + term
                    else:
                        if r == 0:
                            out = out * keep_south
                        if r == TILES - 1:
                            out = out * keep_north
                        dst[f * 4 + l, 8 * r : 8 * r + 8, :] = out
                if last:
                    for o in range(NO):
                        oacc[o, 8 * r - 8 : 8 * r, :] += sums[o]
            return carry

        lax.fori_loop(0, 4, level, 0)
    for n in range(NF):
        late[n // 2, 4 + n % 2] = var[n]
    spread = obsvar[...]
    pm[...] = (spread * obs[...] + oacc[...]) / spread


def adjoint_kernel(
    late_in, dual, follow, fhalo, winds, obs, south, north, west, east, diffusion, weight,
    late, wind, ya, yb, ob,
):
    strips = [strip_of(west, east, t) for t in range(2)]
    load_winds(winds, south, north, strips, wind)
    for o in range(NO):
        load_field(ob, o, O0 + o, obs[o], south, north, strips)
    for f in range(NF):
        start = weight[0, f // 4, f % 4] * ob[0] + weight[1, f // 4, f % 4] * ob[1]
        ya[f, 0:8, :LANES] = start[0:8, :LANES] - fhalo[f]
        ya[f, 8 : 8 + ROWS, :LANES] = start[8 : 8 + ROWS, :LANES] - follow[f]
        ya[f, 8 + ROWS :, :LANES] = start[8 + ROWS :, :LANES] - fhalo[NF + f]
        for r in range(TILES):
            ya[f, 8 * r : 8 * r + 8, LANES:] = start[
                8 * r : 8 * r + 8, LANES:
            ] - unpack_columns(fhalo[2 * NF + r], f)
    keep_south = south[D0, 0:1, 0:1]
    keep_north = north[D0, 7:8, 0:1]
    bufs = (ya, yb)
    for step in range(3):
        s = 2 - step
        src, dst = bufs[step % 2], bufs[(step + 1) % 2]
        last = step == 2

        def level(l, carry, s=s, src=src, dst=dst, last=last):
            for r in range(1, TILES - 1) if last else range(TILES):
                a = wind[s * 8 + l, 8 * r : 8 * r + 8, :]
                b, bn, bs = rows_shifted(wind, s * 8 + 4 + l, r, TILES)
                pa, na = jnp.maximum(a, 0.0), jnp.minimum(a, 0.0)
                base = 1.0 - (pa - na) - jnp.abs(b)
                pbn = jnp.maximum(bn, 0.0)
                nbs = jnp.minimum(bs, 0.0)
                for f in range(4):
                    k = diffusion[f, l]
                    center, yn, ys = rows_shifted(src, f * 4 + l, r, TILES)
                    east_of, _ = from_sides((pa + k) * center)
                    _, west_of = from_sides((k - na) * center)
                    out = (
                        (base - 4.0 * k) * center
                        + east_of
                        + west_of
                        + (pbn + k) * yn
                        + (k - nbs) * ys
                    )
                    if last:
                        rows = slice(8 * r - 8, 8 * r)
                        late[f * 2 + l // 2, 2 + l % 2, rows, :] = (
                            out[:, :LANES] + dual[f * 4 + l, rows, :]
                        )
                    else:
                        if r == 0:
                            out = out * keep_south
                        if r == TILES - 1:
                            out = out * keep_north
                        dst[f * 4 + l, 8 * r : 8 * r + 8, :] = out
            return carry

        lax.fori_loop(0, 4, level, 0)


def ratio(inner, square):
    live = square > 0.0
    return jnp.where(live, inner / jnp.where(live, square, 1.0), 0.0)


def total_of(x):
    return jnp.sum(x, keepdims=True)


def share(inner, square, remain):
    lane = lax.broadcasted_iota(jnp.int32, (8, LANES), 1)
    return jnp.where(
        lane == 0, inner, jnp.where(lane == 1, square, jnp.where(lane == 2, remain, 0.0))
    )


def combine(t):
    lane = lax.broadcasted_iota(jnp.int32, t.shape, 1) == 0
    inner = jnp.where(lane, t, 0.0)
    square = jnp.where(lane, pltpu.roll(t, LANES - 1, 1), 0.0)
    remain = jnp.where(lane, pltpu.roll(t, LANES - 2, 1), 0.0)
    inner_sum, square_sum = total_of(inner), total_of(square)
    d = ratio(inner_sum, square_sum) - ratio(inner, square)
    return inner_sum, square_sum, total_of(remain + square * d * d)


def scan_kernel(windows, late, back):
    def tile(r, carry):
        rows = pl.ds(pl.multiple_of(r * 8, 8), 8)
        for c in range(2):
            run = jnp.zeros((8, LANES), jnp.float32)
            sums = [None] * windows
            for v in reversed(range(windows)):
                run = run + late[v, 2 + c, rows, :]
                sums[v] = run
                back[v, c, rows, :] = run
            run = jnp.zeros((8, LANES), jnp.float32)
            for v in range(windows):
                run = run + (late[v, c, rows, :] - late[v, 4 + c, rows, :] * sums[v])
                back[v, 2 + c, rows, :] = run
        return carry

    lax.fori_loop(0, ROWS // 8, tile, 0)


def dots_kernel(back, moved, dual, inc, pm, obs, shares, px, wv, vv, rr):
    windows = back.shape[0]
    per = NF // windows
    rr[...] = jnp.zeros_like(rr)

    def tile(r, carry):
        rows = pl.ds(pl.multiple_of(r * 8, 8), 8)
        total = jnp.zeros((8, LANES), jnp.float32)
        for half in range(2):
            pairs = [(pm[half, rows, :], obs[half, rows, :])]
            for f in range(half * NF // 2, (half + 1) * NF // 2):
                j, c = f // per, f % per
                x = back[j, per + c, rows, :] + moved[f, rows, :]
                px[f, rows, :] = x
                pairs.append((back[j, c, rows, :], dual[f, rows, :]))
                pairs.append((x, inc[f, rows, :]))
            inner = functools.reduce(jnp.add, [p * x for p, x in pairs])
            square = functools.reduce(jnp.add, [x * x for _, x in pairs])
            h = ratio(inner, square)
            for p, x in pairs:
                d = p - h * x
                total = total + d * d
            wv[2 * r + half] = inner
            vv[2 * r + half] = square
        rr[...] += total
        return carry

    lax.fori_loop(0, ROWS // 8, tile, 0)
    inner, square = wv[...], vv[...]
    h = ratio(inner, square)
    inner_sum = total_of(jnp.sum(inner, 0))
    square_sum = total_of(jnp.sum(square, 0))
    d = ratio(inner_sum, square_sum) - h
    remain = total_of(rr[...] + jnp.sum(square * d * d, 0))
    one = share(inner_sum, square_sum, remain)
    for r in range(shares.shape[0] // 8):
        shares[8 * r : 8 * r + 8, :] = one


def final_kernel(
    count, shares, back, px, dual, inc, pm, obs, o_dual, o_obs, o_inc, coeffs, dv, iv, sems
):
    windows = back.shape[0]
    per = NF // windows
    inner, square, remain = combine(shares[...])
    h = inner / square
    scale = jnp.sqrt(remain / count + 1e-06)
    inv = 1.0 / scale
    first = (lax.broadcasted_iota(jnp.int32, (8, LANES), 0) == 0) & (
        lax.broadcasted_iota(jnp.int32, (8, LANES), 1) == 0
    )
    coeffs[0] = jnp.sum(jnp.where(first, h, 0.0))
    coeffs[1] = jnp.sum(jnp.where(first, scale, 0.0))
    o_obs[...] = (pm[...] - h * obs[...]) * inv
    stores = []
    for n in range(4):
        for f in range(4 * n, 4 * n + 4):
            dv[f] = (back[f // per, f % per] - h * dual[f]) * inv
            iv[f] = (px[f] - h * inc[f]) * inv
        part = slice(4 * n, 4 * n + 4)
        for m, (src, dst) in enumerate(((dv, o_dual), (iv, o_inc))):
            copy = pltpu.make_async_copy(src.at[part], dst.at[part], sems.at[n, m])
            copy.start()
            stores.append(copy)
    for copy in stores:
        copy.wait()


def dma(*shape):
    return pltpu.SemaphoreType.DMA(shape)


def block(*shape, at):
    return pl.BlockSpec(shape, lambda i: at)


def across(x, axes):
    return lax.all_to_all(x, axes, 0, 0, tiled=True)


def iteration(dual, obs_dual, increment, trajectory, diffusion, obs_weight, model_var, obs_var):
    windows = lax.axis_size("win")
    columns = lax.axis_size("tx")
    ranks = lax.axis_size("ty")
    devices = windows * columns * ranks
    per = NF // windows
    tied = lax.optimization_barrier
    lam = dual.reshape(NF, ROWS, LANES)
    inc = increment.reshape(NF, ROWS, LANES)
    winds = trajectory.reshape(NW, ROWS, LANES)
    obs = obs_dual.reshape(NO, ROWS, LANES)
    var = model_var.reshape(NF, ROWS, LANES)
    obsvar = obs_var.reshape(NO, ROWS, LANES)
    to_previous = [(i + 1, i) for i in range(windows - 1)]

    every = (lam, inc, winds, obs)
    last = ROWS // 8 - 1
    top, bottom = pl.pallas_call(
        edges_kernel,
        grid=(1,),
        out_shape=(vmem(ALL, 8, LANES), vmem(ALL, 8, LANES)),
        in_specs=[block(x.shape[0], 8, LANES, at=(0, 0, 0)) for x in every]
        + [block(x.shape[0], 8, LANES, at=(0, last, 0)) for x in every],
        out_specs=[VM, VM],
        compiler_params=GRANT,
        name="edges",
    )(*(far(x) for x in every + every))
    south = held(lax.ppermute(bottom, "ty", [(i, i + 1) for i in range(ranks - 1)]))
    north = held(lax.ppermute(top, "ty", [(i + 1, i) for i in range(ranks - 1)]))
    packed = pl.pallas_call(
        pack_kernel,
        out_shape=vmem(ROWS, 3 * LANES),
        in_specs=[VM] * 4,
        out_specs=VM,
        compiler_params=GRANT,
        name="pack",
    )(*(held(x) for x in every))
    full = pl.pallas_call(
        edges_halo_kernel,
        out_shape=vmem(EXT, 3 * LANES),
        in_specs=[VM] * 3,
        out_specs=VM,
        compiler_params=GRANT,
        name="edges_halo",
    )(south, north, packed)
    full, lam_out = tied((full, lam))
    ring = [(i, (i + 1) % columns) for i in range(columns)]
    west = held(lax.ppermute(full, "tx", ring))
    east = held(lax.ppermute(full, "tx", [(j, i) for i, j in ring]))
    follow = held(lax.ppermute(lam_out, "win", to_previous))

    fhalo = pl.pallas_call(
        follow_halo_kernel,
        out_shape=vmem(2 * NF + TILES, 8, LANES),
        in_specs=[VM] * 4,
        out_specs=VM,
        compiler_params=GRANT,
        name="follow_halo",
    )(south, north, west, east)
    fhalo = held(lax.ppermute(fhalo, "win", to_previous))

    field = vmem(NF, EXT, 2 * LANES)
    wind = vmem(NW, EXT, 2 * LANES)
    late, moved, pm = pl.pallas_call(
        forward_kernel,
        out_shape=(
            vmem(windows, 3 * per, ROWS, LANES),
            vmem(NF, ROWS, LANES),
            vmem(NO, ROWS, LANES),
        ),
        in_specs=[VM] * 10 + [SM] * 2,
        out_specs=(VM, VM, VM),
        scratch_shapes=[wind, field, field, vmem(NO, ROWS, LANES)],
        compiler_params=GRANT,
        name="forward",
    )(held(inc), held(lam), held(var), held(winds), held(obs), held(obsvar), south, north, west, east, diffusion, obs_weight)
    late = pl.pallas_call(
        adjoint_kernel,
        out_shape=vmem(windows, 3 * per, ROWS, LANES),
        in_specs=[VM] * 10 + [SM] * 2,
        out_specs=VM,
        scratch_shapes=[wind, field, field, vmem(NO, EXT, 2 * LANES)],
        input_output_aliases={0: 0},
        compiler_params=GRANT,
        name="adjoint",
    )(late, held(lam), follow, fhalo, held(winds), held(obs), south, north, west, east, diffusion, obs_weight)

    late = held(across(late, "win"))
    tiles = 2 * ROWS // 8
    back = pl.pallas_call(
        functools.partial(scan_kernel, windows),
        out_shape=vmem(windows, 2 * per, ROWS, LANES),
        in_specs=[VM],
        out_specs=VM,
        compiler_params=GRANT,
        name="scans",
    )(late)
    back = held(across(back, "win"))
    shares, px = pl.pallas_call(
        dots_kernel,
        out_shape=(vmem(devices, LANES), vmem(NF, ROWS, LANES)),
        in_specs=[VM] * 6,
        out_specs=(VM, VM),
        scratch_shapes=[vmem(tiles, 8, LANES), vmem(tiles, 8, LANES), vmem(8, LANES)],
        compiler_params=GRANT,
        name="dots",
    )(back, moved, held(lam), held(inc), pm, held(obs))
    shares = across(shares, ("win", "tx", "ty"))
    count = float((2 * NF + NO) * ROWS * LANES * devices)
    o_dual, o_obs, o_inc, coeffs = pl.pallas_call(
        functools.partial(final_kernel, count),
        out_shape=(sds(NF, ROWS, LANES), sds(NO, ROWS, LANES), sds(NF, ROWS, LANES), sds(2)),
        in_specs=[VM] * 7,
        out_specs=(HB, VM, HB, SM),
        scratch_shapes=[vmem(NF, ROWS, LANES), vmem(NF, ROWS, LANES), dma(4, 2)],
        compiler_params=GRANT,
        name="final",
    )(held(shares), back, px, held(lam), held(inc), pm, held(obs))
    return (
        o_dual.reshape(dual.shape),
        o_obs.reshape(obs_dual.shape),
        o_inc.reshape(increment.shape),
        coeffs,
    )


def solution(mesh):
    in_specs = (
        P("win", None, None, "ty", "tx"),
        P("win", None, "ty", "tx"),
        P("win", None, None, "ty", "tx"),
        P("win", None, None, None, "ty", "tx"),
        P(),
        P(),
        P("win", None, None, "ty", "tx"),
        P("win", None, "ty", "tx"),
    )
    out_specs = (
        P("win", None, None, "ty", "tx"),
        P("win", None, "ty", "tx"),
        P("win", None, None, "ty", "tx"),
        P(),
    )
    return jax.shard_map(
        iteration, mesh=mesh, in_specs=in_specs, out_specs=out_specs, check_vma=False
    )
```

time: 132 us -> 111 us (0.84)
  Pallas kernels: 24.4 us -> 14.8 us
  blocking collectives: 61 us -> 69.8 us
  starting transfers between devices: 20.6 us -> 14.8 us
  waiting for transfers between devices: 15 us -> 10.5 us
  other arithmetic: 4.47 us -> 0 us
  local copies, waits for them, and re-layouts: 4.5 us -> 0.04 us
    pallas_call x6 -> x9, Pallas kernels: 24.4 us -> 14.8 us  [the longest x1 4.64 us: iteration(): pl.pallas_call(adjoint_kernel, out_shape=vmem(windows, 3 * per, ROWS, LAN...]
    all_to_all x3, blocking collectives: 61 us -> 69.8 us  [across(): return lax.all_to_all(x, axes, 0, 0, tiled=True)]
    all_to_all x1 -> x0, starting transfers between devices: 7.47 us -> none  [per_device(): early = lax.all_to_all(early, 'win', 0, 0)]
    ppermute x6, waiting for transfers between devices: 15 us -> 10.5 us  [the longest x1 4.41 us: iteration(): lax.ppermute(top, 'ty', [(i + 1, i) for i in range(ranks - 1)])]
    concatenate x3 -> x0, other arithmetic: 3.86 us -> none  [the longest x1 2.71 us: per_device(): jnp.concatenate([x.reshape(windows, NF // windows, ROWS, LANES) for x in...]
    unnamed x20 -> x16, local copies, waits for them, and re-layouts: 2.17 us -> 0.04 us
    slice x2 -> x0, local copies, waits for them, and re-layouts: 1.69 us -> none  [the longest x1 0.84 us: per_device(): south[ALL - NF:]]
    ppermute x6, starting transfers between devices: 13.1 us -> 14.8 us  [the longest x1 5.65 us: iteration(): east = held(lax.ppermute(full, 'tx', [(j, i) for i, j in ring]))]
  transfers between devices with their start and end apart: 7 -> 6, of which waited for: 4 -> 4; matrix products, arithmetic and copies ran while one was open for 3% -> 0% of each run, Pallas kernels for 14% -> 5%
where the time goes in v2:
time: 111 us
  blocking collectives  69.8 us (63%)
  Pallas kernels  14.8 us (13%)
  starting transfers between devices  14.8 us (13%)
  waiting for transfers between devices  10.5 us (9%)
    all_to_all x3, blocking collectives, across(): return lax.all_to_all(x, axes, 0, 0, tiled=True)  69.8 us
    ppermute x1, starting transfers between devices, iteration(): east = held(lax.ppermute(full, 'tx', [(j, i) for i, j in ring]))  5.65 us
    pallas_call x1, Pallas kernels, iteration(): pl.pallas_call(adjoint_kernel, out_shape=vmem(windows, 3 * per, ROWS, LAN...  4.64 us
    ppermute x1, starting transfers between devices, iteration(): lax.ppermute(bottom, 'ty', [(i, i + 1) for i in range(ranks - 1)])  4.5 us
    ppermute x1, waiting for transfers between devices, iteration(): lax.ppermute(top, 'ty', [(i + 1, i) for i in range(ranks - 1)])  4.41 us
    pallas_call x1, Pallas kernels, iteration(): pl.pallas_call(forward_kernel, out_shape=(vmem(windows, 3 * per, ROWS, LA...  4.32 us
    ppermute x1, waiting for transfers between devices, iteration(): west = held(lax.ppermute(full, 'tx', ring))  3.07 us
  transfers between devices with their start and end apart: 6, of which 4 were waited for; matrix products, arithmetic and copies ran while one was open for 0% of the time, Pallas kernels for 5%

profile of v2, /device:TPU:1, one launch (start us, length us, event | category | flops | bytes accessed | tf_op | source)
XLA Modules:
  0.0 110.8 jit_solution(2907045247974048094)
XLA Ops:
  0.7 1.3 %edges.1 = (f32[58,8,128]{2,1,0:T(8,128)S(1)}, f32[58,8,128]{2,1,0:T(8,128)S(1)}) custom-call(f32[16,64,128]{2,1,0:T(8,128)} %bitcast.13, f32[16,64,128]{2,1,0:T(8,128)} %bitcast.26, f32[24,64,128]{2,1,0:T(8,128)} %bitcast.21, f32[2,64,128]{2,1,0:T(8,128)} %bitcast.32, f32[16,64,128]{2,1,0:T(8,128)} %bitcast.14, f32[16,64,128]{2,1,0:T(8,128)} %bitcast.27, ...), custom_call_target="tpu_custom_call" | custom-call | tf_op jit(solution)/shard_map/edges/pallas_call | solution.py:414
  1.9 4.5 %collective-permute-start = (f32[58,8,128]{2,1,0:T(8,128)S(1)}, f32[58,8,128]{2,1,0:T(8,128)S(1)}, u32[]{:S(2)}, u32[]{:S(2)}) collective-permute-start(f32[58,8,128]{2,1,0:T(8,128)S(1)} %get-tuple-element.17), channel_id=1, source_target_pairs={{0,1},{1,2},{2,3},{4,5},{5,6},{6,7},{8,9},{9,10},{10,11},{12,13},{... | collective-permute-start | bytes 712712 | tf_op jit(solution)/shard_map/ppermute | solution.py:424
  6.4 0.0 copy-start.4
  6.4 0.0 copy-start.5
  6.5 0.0 copy-start.6
  6.5 0.0 copy-start.7
  6.5 2.1 %collective-permute-start.1 = (f32[58,8,128]{2,1,0:T(8,128)S(1)}, f32[58,8,128]{2,1,0:T(8,128)S(1)}, u32[]{:S(2)}, u32[]{:S(2)}) collective-permute-start(f32[58,8,128]{2,1,0:T(8,128)S(1)} %get-tuple-element.18), channel_id=1, source_target_pairs={{1,0},{2,1},{3,2},{5,4},{6,5},{7,6},{9,8},{10,9},{11,10},{13,12},{... | collective-permute-start | bytes 712712 | tf_op jit(solution)/shard_map/ppermute | solution.py:425
  8.6 1.0 pack.1.packed
  9.6 4.4 %collective-permute-done.1.north = f32[58,8,128]{2,1,0:T(8,128)S(1)} collective-permute-done((f32[58,8,128]{2,1,0:T(8,128)S(1)}, f32[58,8,128]{2,1,0:T(8,128)S(1)}, u32[]{:S(2)}, u32[]{:S(2)}) %collective-permute-start.1) | collective-permute-done | bytes 237600 | tf_op jit(solution)/shard_map/ppermute | solution.py:425
  14.0 0.2 edges_halo.1
  14.2 1.3 %collective-permute-start.4 = (f32[16,64,128]{2,1,0:T(8,128)S(1)}, f32[16,64,128]{2,1,0:T(8,128)S(1)}, u32[]{:S(2)}, u32[]{:S(2)}) collective-permute-start(f32[16,64,128]{2,1,0:T(8,128)S(1)} %bitcast.16), channel_id=1, source_target_pairs={{32,0},{64,32},{96,64},{128,96},{160,128},{192,160},{224,192},{33,... | collective-permute-start | bytes 1572872 | tf_op jit(solution)/shard_map/ppermute | solution.py:446
  15.5 5.7 %collective-permute-start.3 = (f32[80,384]{1,0:T(8,128)S(1)}, f32[80,384]{1,0:T(8,128)S(1)}, u32[]{:S(2)}, u32[]{:S(2)}) collective-permute-start(f32[80,384]{1,0:T(8,128)S(1)} %edges_halo.1), channel_id=1, source_target_pairs={{4,0},{8,4},{12,8},{16,12},{20,16},{24,20},{28,24},{0,28},{5,1},{9... | collective-permute-start | bytes 368648 | tf_op jit(solution)/shard_map/ppermute | solution.py:445
  21.2 1.9 %collective-permute-done.3.east = f32[80,384]{1,0:T(8,128)S(1)} collective-permute-done((f32[80,384]{1,0:T(8,128)S(1)}, f32[80,384]{1,0:T(8,128)S(1)}, u32[]{:S(2)}, u32[]{:S(2)}) %collective-permute-start.3) | collective-permute-done | bytes 122912 | tf_op jit(solution)/shard_map/ppermute | solution.py:445
  23.1 3.1 %collective-permute-done.2.west = f32[80,384]{1,0:T(8,128)S(1)} collective-permute-done((f32[80,384]{1,0:T(8,128)S(1)}, f32[80,384]{1,0:T(8,128)S(1)}, u32[]{:S(2)}, u32[]{:S(2)}) %collective-permute-start.2) | collective-permute-done | bytes 122912 | tf_op jit(solution)/shard_map/ppermute | solution.py:444
  26.1 1.3 %collective-permute-start.5 = (f32[42,8,128]{2,1,0:T(8,128)S(1)}, f32[42,8,128]{2,1,0:T(8,128)S(1)}, u32[]{:S(2)}, u32[]{:S(2)}) collective-permute-start(f32[42,8,128]{2,1,0:T(8,128)S(1)} %follow_halo.1), channel_id=1, source_target_pairs={{32,0},{64,32},{96,64},{128,96},{160,128},{192,160},{224,192},{33,... | collective-permute-start | bytes 516104 | tf_op jit(solution)/shard_map/ppermute | solution.py:456
  27.5 4.3 %forward.1 = (f32[8,6,64,128]{3,2,1,0:T(8,128)S(1)}, f32[16,64,128]{2,1,0:T(8,128)S(1)}, f32[2,64,128]{2,1,0:T(8,128)S(1)}) custom-call(f32[16,64,128]{2,1,0:T(8,128)S(1)} %bitcast.29, f32[16,64,128]{2,1,0:T(8,128)S(1)} %bitcast.17, f32[16,64,128]{2,1,0:T(8,128)S(1)} %bitcast.40, f32[24,64,128]{2,1,0:T(8,128)S(1)} %bitcast.24, f32[2,64,128]{2,1,0:T(8,128)S(1)} %bitcast.35, ...), custom_call_target="tpu_custom_call" | custom-call | tf_op jit(solution)/shard_map/forward/pallas_call | solution.py:460
  31.8 1.1 %collective-permute-done.5.fhalo = f32[42,8,128]{2,1,0:T(8,128)S(1)} collective-permute-done((f32[42,8,128]{2,1,0:T(8,128)S(1)}, f32[42,8,128]{2,1,0:T(8,128)S(1)}, u32[]{:S(2)}, u32[]{:S(2)}) %collective-permute-start.5) | collective-permute-done | bytes 172064 | tf_op jit(solution)/shard_map/ppermute | solution.py:456
  32.9 4.6 %adjoint.1 = f32[8,6,64,128]{3,2,1,0:T(8,128)S(1)} custom-call(f32[8,6,64,128]{3,2,1,0:T(8,128)S(1)} %get-tuple-element.20.late_in, f32[16,64,128]{2,1,0:T(8,128)S(1)} %bitcast.18, f32[16,64,128]{2,1,0:T(8,128)S(1)} %collective-permute-done.4.follow, f32[42,8,128]{2,1,0:T(8,128)S(1)} %collective-permute-done.5.fhalo, ...), custom_call_target="tpu_custom_call", output_to_operand_aliasing={{}: (0, {})} | custom-call | tf_op jit(solution)/shard_map/adjoint/pallas_call | solution.py:473
  37.6 30.2 %all_to_all.21.late = f32[8,6,64,128]{3,2,1,0:T(8,128)S(1)} all-to-all(f32[8,6,64,128]{3,2,1,0:T(8,128)S(1)} %adjoint.1), channel_id=1, replica_groups=mesh['win'=8,'tx'=8,'ty'=4] {'win'}, dimensions={0} | all-to-all | bytes 3145728 | tf_op jit(solution)/shard_map/all_to_all | solution.py:394
  67.8 0.3 scans.1
  68.1 18.5 %all_to_all.22.back = f32[8,4,64,128]{3,2,1,0:T(8,128)S(1)} all-to-all(f32[8,4,64,128]{3,2,1,0:T(8,128)S(1)} %scans.1), channel_id=1, replica_groups=mesh['win'=8,'tx'=8,'ty'=4] {'win'}, dimensions={0} | all-to-all | bytes 2097152 | tf_op jit(solution)/shard_map/all_to_all | solution.py:394
  86.6 1.0 dots.1
  87.6 21.1 %all_to_all.23 = f32[256,1,128]{2,1,0:T(1,128)S(1)} all-to-all(f32[256,1,128]{2,1,0:T(1,128)S(1)} %bitcast.41), channel_id=1, replica_groups=mesh['win'=8,'tx'=8,'ty'=4] {'win','tx','ty'}, dimensions={0} | all-to-all | bytes 262144 | tf_op jit(solution)/shard_map/all_to_all | solution.py:394
  108.6 2.1 %final.1 = (f32[16,64,128]{2,1,0:T(8,128)}, f32[2,64,128]{2,1,0:T(8,128)}, f32[16,64,128]{2,1,0:T(8,128)}, f32[2]{0:T(128)}) custom-call(f32[256,128]{1,0:T(8,128)S(1)} %bitcast.39, f32[8,4,64,128]{3,2,1,0:T(8,128)S(1)} %all_to_all.22.back, f32[16,64,128]{2,1,0:T(8,128)S(1)} %get-tuple-element.25.px, f32[16,64,128]{2,1,0:T(8,128)S(1)} %bitcast.20, ...), custom_call_target="tpu_custom_call" | custom-call | tf_op jit(solution)/shard_map/final/pallas_call | solution.py:506
  (16 shorter events, 0.0 us)
Async XLA Ops:
  0.6 7.9 %copy-start = (f32[1,4,4,64,128]{4,3,2,1,0:T(8,128)S(1)}, f32[1,4,4,64,128]{4,3,2,1,0:T(8,128)}, u32[]{:S(2)}) copy-start(f32[1,4,4,64,128]{4,3,2,1,0:T(8,128)} %param.8) | copy-start | bytes 1572868
  0.6 7.9 %copy-start.1 = (f32[1,3,2,4,64,128]{5,4,3,2,1,0:T(8,128)S(1)}, f32[1,3,2,4,64,128]{5,4,3,2,1,0:T(8,128)}, u32[]{:S(2)}) copy-start(f32[1,3,2,4,64,128]{5,4,3,2,1,0:T(8,128)} %param.11) | copy-start | bytes 2359300
  0.7 7.9 %copy-start.2 = (f32[1,4,4,64,128]{4,3,2,1,0:T(8,128)S(1)}, f32[1,4,4,64,128]{4,3,2,1,0:T(8,128)}, u32[]{:S(2)}) copy-start(f32[1,4,4,64,128]{4,3,2,1,0:T(8,128)} %param.10) | copy-start | bytes 1572868
  0.7 7.9 %copy-start.3 = (f32[1,2,64,128]{3,2,1,0:T(8,128)S(1)}, f32[1,2,64,128]{3,2,1,0:T(8,128)}, u32[]{:S(2)}) copy-start(f32[1,2,64,128]{3,2,1,0:T(8,128)} %param.9) | copy-start | bytes 196612
  1.9 7.7 %collective-permute-start = (f32[58,8,128]{2,1,0:T(8,128)S(1)}, f32[58,8,128]{2,1,0:T(8,128)S(1)}, u32[]{:S(2)}, u32[]{:S(2)}) collective-permute-start(f32[58,8,128]{2,1,0:T(8,128)S(1)} %get-tuple-element.17), channel_id=1, source_target_pairs={{0,1},{1,2},{2,3},{4,5},{5,6},{6,7},{8,9},{9,10},{10,11},{12,13},{... | collective-permute-start | bytes 712712 | tf_op jit(solution)/shard_map/ppermute | solution.py:424
  6.4 21.0 %copy-start.4 = (f32[1,4,4,64,128]{4,3,2,1,0:T(8,128)S(1)}, f32[1,4,4,64,128]{4,3,2,1,0:T(8,128)}, u32[]{:S(2)}) copy-start(f32[1,4,4,64,128]{4,3,2,1,0:T(8,128)} %param.14) | copy-start | bytes 1572868
  6.4 21.0 %copy-start.5 = (f32[1,2,64,128]{3,2,1,0:T(8,128)S(1)}, f32[1,2,64,128]{3,2,1,0:T(8,128)}, u32[]{:S(2)}) copy-start(f32[1,2,64,128]{3,2,1,0:T(8,128)} %param.15) | copy-start | bytes 196612
  6.5 21.0 %copy-start.6 = (f32[2,4,4]{2,1,0:T(4,128)S(1)}, f32[2,4,4]{2,1,0:T(4,128)}, u32[]{:S(2)}) copy-start(f32[2,4,4]{2,1,0:T(4,128)} %weight.3) | copy-start | bytes 388
  6.5 21.0 %copy-start.7 = (f32[4,4]{1,0:T(4,128)S(1)}, f32[4,4]{1,0:T(4,128)}, u32[]{:S(2)}) copy-start(f32[4,4]{1,0:T(4,128)} %diffusion.3) | copy-start | bytes 196
  6.5 7.6 %collective-permute-start.1 = (f32[58,8,128]{2,1,0:T(8,128)S(1)}, f32[58,8,128]{2,1,0:T(8,128)S(1)}, u32[]{:S(2)}, u32[]{:S(2)}) collective-permute-start(f32[58,8,128]{2,1,0:T(8,128)S(1)} %get-tuple-element.18), channel_id=1, source_target_pairs={{1,0},{2,1},{3,2},{5,4},{6,5},{7,6},{9,8},{10,9},{11,10},{13,12},{... | collective-permute-start | bytes 712712 | tf_op jit(solution)/shard_map/ppermute | solution.py:425
  14.2 18.7 %collective-permute-start.4 = (f32[16,64,128]{2,1,0:T(8,128)S(1)}, f32[16,64,128]{2,1,0:T(8,128)S(1)}, u32[]{:S(2)}, u32[]{:S(2)}) collective-permute-start(f32[16,64,128]{2,1,0:T(8,128)S(1)} %bitcast.16), channel_id=1, source_target_pairs={{32,0},{64,32},{96,64},{128,96},{160,128},{192,160},{224,192},{33,... | collective-permute-start | bytes 1572872 | tf_op jit(solution)/shard_map/ppermute | solution.py:446
  15.5 7.5 %collective-permute-start.3 = (f32[80,384]{1,0:T(8,128)S(1)}, f32[80,384]{1,0:T(8,128)S(1)}, u32[]{:S(2)}, u32[]{:S(2)}) collective-permute-start(f32[80,384]{1,0:T(8,128)S(1)} %edges_halo.1), channel_id=1, source_target_pairs={{4,0},{8,4},{12,8},{16,12},{20,16},{24,20},{28,24},{0,28},{5,1},{9... | collective-permute-start | bytes 368648 | tf_op jit(solution)/shard_map/ppermute | solution.py:445
  21.2 4.9 %collective-permute-start.2 = (f32[80,384]{1,0:T(8,128)S(1)}, f32[80,384]{1,0:T(8,128)S(1)}, u32[]{:S(2)}, u32[]{:S(2)}) collective-permute-start(f32[80,384]{1,0:T(8,128)S(1)} %edges_halo.1), channel_id=1, source_target_pairs={{0,4},{4,8},{8,12},{12,16},{16,20},{20,24},{24,28},{28,0},{1,5},{5... | collective-permute-start | bytes 368648 | tf_op jit(solution)/shard_map/ppermute | solution.py:444
  26.1 6.8 %collective-permute-start.5 = (f32[42,8,128]{2,1,0:T(8,128)S(1)}, f32[42,8,128]{2,1,0:T(8,128)S(1)}, u32[]{:S(2)}, u32[]{:S(2)}) collective-permute-start(f32[42,8,128]{2,1,0:T(8,128)S(1)} %follow_halo.1), channel_id=1, source_target_pairs={{32,0},{64,32},{96,64},{128,96},{160,128},{192,160},{224,192},{33,... | collective-permute-start | bytes 516104 | tf_op jit(solution)/shard_map/ppermute | solution.py:456
